TPU v7x, 128 devices: a whole 4x4x4 slice. The times are simulated.
128 devices in a mesh: lat: 16 (over y, z), lon: 8 (over x, core).
Axes of the slice: x: 4, y: 4, z: 4, core: 2. Of those that a mesh axis runs over, the one named last changes fastest.
Arguments:
- fields: bfloat16 [1, 1024, 512, 384], P(None, 'lat', 'lon'), may hold values from -6 to 6
- land: int32 [1024, 512], P('lat', 'lon'), may hold values from 0 to 1
- norm_gains: float32 [4, 384], replicated, may hold values from 0.1 to 1.9
- qkv_weight: bfloat16 [2, 384, 1152], replicated, may hold values from -9 to 9
- rel_bias: float32 [2, 12, 225], replicated, may hold values from -4 to 4
- proj_weight: bfloat16 [2, 384, 384], replicated, may hold values from -0.3125 to 0.3125
- up_weight: bfloat16 [2, 384, 1536], replicated, may hold values from -0.3125 to 0.3125
- down_weight: bfloat16 [2, 1536, 384], replicated, may hold values from -0.15625 to 0.15625
Outputs:
- evolved: bfloat16 [1, 1024, 512, 384], P(None, 'lat', 'lon')
All inputs are finite; a program needn't handle non-finite values.
Results may differ from a plain program's by a relative error of at most 0.013.
Values may be sent and summed in bfloat16 or wider, within the bound.
No kernel may reach another device: no remote copies, remote signals or barrier semaphores. Data moves between devices by JAX's collectives and lax.ppermute only.
A program may use at most 256 MiB of HBM per device.

v0:
```python
import functools

import jax
import jax.numpy as jnp
import numpy as np
from jax import lax
from jax.experimental import pallas as pl
from jax.experimental.pallas import tpu as pltpu
from jax.sharding import PartitionSpec as P

HEADS = 12
WIN = 8
SHIFT = 4
EPS = 1e-05
C = 384
HID = 1536
TOK = WIN * WIN
BIG = 1e30
LOG2E = 1.4426950408889634
QSCALE = LOG2E / (C // HEADS) ** 0.5
BF = jnp.bfloat16
F32 = jnp.float32


def places(shifted):
    slot = np.arange(TOK)
    col = slot % WIN
    return slot // WIN, (col + SHIFT) % WIN if shifted else col


def bias_selector(shifted):
    row, col = places(shifted)
    index = (row[None, :] - row[:, None] + WIN - 1) * (2 * WIN - 1) + (col[None, :] - col[:, None] + WIN - 1)
    index = np.concatenate([index, index], axis=1).reshape(-1)
    table = np.zeros(((2 * WIN - 1) ** 2, index.size), np.float32)
    table[index, np.arange(index.size)] = 1.0
    return table


def bias_tiles(table, shifted):
    table = table * LOG2E
    high = table.astype(BF)
    low = (table - high.astype(F32)).astype(BF)
    both = jnp.concatenate([high, low], axis=0)
    picked = jnp.dot(both, jnp.asarray(bias_selector(shifted), BF), preferred_element_type=F32)
    return (picked[:HEADS] + picked[HEADS:]).reshape(HEADS, TOK, 2 * TOK)


def flag_matrices(windows, tiles, shifted):
    slot = np.arange(TOK) % WIN
    lane = np.arange(128)
    match = (lane[None, :] % WIN == slot[:, None]) & (lane[None, :] < tiles * WIN)
    win = np.repeat(np.arange(windows), TOK)
    if not shifted:
        return match.astype(np.float32), (lane[:, None] // WIN == win[None, :]).astype(np.float32)
    low = match & (slot[:, None] < SHIFT)
    high = match & (slot[:, None] >= SHIFT)
    spread = np.concatenate([low, high], axis=1).astype(np.float32)
    pick_low = lane[:, None] // WIN == win[None, :] % tiles
    pick_high = lane[:, None] // WIN == (win[None, :] - 1) % tiles
    return spread, np.concatenate([pick_low, pick_high], axis=0).astype(np.float32)


def normed(values, gain):
    center = jnp.mean(values, axis=-1, keepdims=True)
    moved = values - center
    spread = jnp.mean(moved * moved, axis=-1, keepdims=True)
    return (moved * lax.rsqrt(spread + EPS) * gain).astype(BF)


def dot_nt(a, b):
    return lax.dot_general(a, b, (((1,), (1,)), ((), ())), preferred_element_type=F32)


def dot_nn(a, b):
    return jnp.dot(a, b, preferred_element_type=F32)


def attend_pair(q_ref, k_ref, vt_ref, bias_ref, mask, first, second):
    lane_head = lax.broadcasted_iota(jnp.int32, (TOK, 128), 1) // 32
    lane = lax.broadcasted_iota(jnp.int32, (TOK, 2 * TOK), 1)
    zero = jnp.zeros((TOK, 128), BF)
    rows = (pl.ds(first * TOK, TOK), pl.ds(second * TOK, TOK))
    if second == first + 1 and first % 2 == 0:
        values = vt_ref[:, pl.ds(first * TOK, 2 * TOK)]
    else:
        values = vt_ref[:, pl.ds(first * TOK, 2 * TOK)]
        values = jnp.concatenate([values[:, :TOK], values[:, :TOK]], axis=1)
    outs = []
    for group in range(3):
        lanes = pl.ds(group * 128, 128)
        keys = jnp.concatenate([k_ref[rows[0], lanes], k_ref[rows[1], lanes]], axis=1)
        q0, q1 = q_ref[rows[0], lanes], q_ref[rows[1], lanes]
        for half in range(2):
            blocks = []
            for head in (2 * half, 2 * half + 1):
                here = lane_head == head
                blocks.append(jnp.concatenate([jnp.where(here, q0, zero), zero], axis=1))
                blocks.append(jnp.concatenate([zero, jnp.where(here, q1, zero)], axis=1))
            scores = dot_nt(keys, jnp.concatenate(blocks, axis=0))
            for j in range(2):
                head = group * 4 + 2 * half + j
                s = scores[:, j * 128 : (j + 1) * 128] + bias_ref[head] + mask
                top = jnp.max(s, axis=0, keepdims=True)
                e = jnp.exp2(s - top)
                total = jnp.sum(e, axis=0, keepdims=True)
                p = (e * (1.0 / total)).astype(BF)
                spread = jnp.concatenate(
                    [jnp.where(lane < TOK, p, jnp.zeros_like(p)), jnp.where(lane < TOK, jnp.zeros_like(p), p)], axis=0
                )
                outs.append(dot_nn(values[head * 32 : (head + 1) * 32], spread))
    return jnp.concatenate(outs, axis=0)


def pair_mask(flags, spread_ref, pick_ref):
    rows = jnp.broadcast_to(flags.astype(F32)[:, None, :], (WIN, WIN, 128)).reshape(TOK, 128)
    if spread_ref.shape[1] == 256:
        rows = jnp.concatenate([rows, rows], axis=1)
    return dot_nn((rows * spread_ref[...]).astype(BF), pick_ref[...]) * -BIG


def finish(x, mixed, proj_ref, gain, up_ref, down_ref):
    mid = (x + dot_nn(mixed, proj_ref[...])).astype(BF).astype(F32)
    hidden = dot_nn(normed(mid, gain), up_ref[...])
    hidden = jax.nn.gelu(hidden, approximate=True).astype(BF)
    return mid + dot_nn(hidden, down_ref[...])


def project(x_win, gain, qkv_ref, wvt_ref, q_ref, k_ref, vt_ref):
    packed = normed(x_win, gain)
    q_ref[...] = (dot_nn(packed, qkv_ref[:, :C]) * QSCALE).astype(BF)
    k_ref[...] = dot_nn(packed, qkv_ref[:, C : 2 * C]).astype(BF)
    vt_ref[...] = dot_nt(wvt_ref[...], packed).astype(BF)


def first_kernel(x_ref, land_ref, gain_ref, qkv_ref, wvt_ref, bias_ref, spread_ref, pick_ref, proj_ref, up_ref, down_ref,
                 out_ref, xw_ref, q_ref, k_ref, vt_ref, o_ref):
    windows = 8
    for r in range(WIN):
        for w in range(windows):
            xw_ref[pl.ds(w * TOK + r * WIN, WIN), :] = x_ref[r, pl.ds(w * WIN, WIN), :].astype(F32)
    project(xw_ref[...], gain_ref[0:1], qkv_ref, wvt_ref, q_ref, k_ref, vt_ref)
    neg = pair_mask(land_ref[...], spread_ref, pick_ref)
    key = lax.broadcasted_iota(jnp.int32, (TOK, 128), 0)
    own = lax.broadcasted_iota(jnp.int32, (TOK, 128), 1) % TOK == key
    for pair in range(windows // 2):
        mask = jnp.where(own, 0.0, neg[:, pair * 128 : (pair + 1) * 128])
        o_ref[pl.ds(pair * 128, 128), :] = attend_pair(q_ref, k_ref, vt_ref, bias_ref, mask, 2 * pair, 2 * pair + 1).astype(BF).T
    result = finish(xw_ref[...], o_ref[...], proj_ref, gain_ref[1:2], up_ref, down_ref)
    for r in range(WIN):
        for w in range(windows):
            out_ref[r, pl.ds(w * WIN, WIN), :] = result[w * TOK + r * WIN : w * TOK + (r + 1) * WIN].astype(BF)


def second_kernel(x_ref, own_ref, land_ref, gain_ref, qkv_ref, wvt_ref, bias_ref, spread_ref, pick_ref, proj_ref, up_ref, down_ref,
                  out_ref, xw_ref, q_ref, k_ref, vt_ref, o_ref, att_ref):
    windows = 9
    step = pl.program_id(0)
    low = lax.broadcasted_iota(jnp.int32, (WIN, C), 0) < SHIFT
    for r in range(WIN):
        tiles = [x_ref[r, pl.ds(t * WIN, WIN), :].astype(F32) for t in range(windows)]
        for w in range(windows):
            xw_ref[pl.ds(w * TOK + r * WIN, WIN), :] = jnp.where(low, tiles[w], tiles[(w - 1) % windows])
    xw_ref[pl.ds(windows * TOK, TOK), :] = jnp.zeros((TOK, C), F32)
    project(xw_ref[...], gain_ref[0:1], qkv_ref, wvt_ref, q_ref, k_ref, vt_ref)
    neg = pair_mask(land_ref[...], spread_ref, pick_ref)
    key = lax.broadcasted_iota(jnp.int32, (TOK, 128), 0)
    own = lax.broadcasted_iota(jnp.int32, (TOK, 128), 1) % TOK == key
    for pair in range(5):
        mask = jnp.where(own, 0.0, neg[:, pair * 128 : (pair + 1) * 128])
        o_ref[pl.ds(pair * 128, 128), :] = attend_pair(q_ref, k_ref, vt_ref, bias_ref, mask, 2 * pair, 2 * pair + 1).T
    for t in range(8):
        for r in range(WIN):
            left = o_ref[pl.ds(t * TOK + r * WIN, WIN), :]
            right = o_ref[pl.ds((t + 1) * TOK + r * WIN, WIN), :]
            att_ref[r + SHIFT, pl.ds(t * WIN, WIN), :] = jnp.where(low, left, right)

    @pl.when(step > 0)
    def _():
        mixed = att_ref[0:WIN].reshape(WIN * 64, C).astype(BF)
        x = own_ref[...].astype(F32).reshape(WIN * 64, C)
        result = finish(x, mixed, proj_ref, gain_ref[1:2], up_ref, down_ref)
        out_ref[...] = result.reshape(WIN, 64, C).astype(BF)

    att_ref[0:SHIFT] = att_ref[WIN : WIN + SHIFT]


def whole(shape):
    return pl.BlockSpec(shape, lambda i: (0,) * len(shape), pipeline_mode=pl.Buffered(1))


def layer_weights(layer, norm_gains, qkv_weight, proj_weight, up_weight, down_weight):
    qkv = qkv_weight[layer]
    return (norm_gains[2 * layer : 2 * layer + 2], qkv, qkv[:, 2 * C :].T, proj_weight[layer], up_weight[layer], down_weight[layer])


def weight_specs():
    return [whole((2, C)), whole((C, 3 * C)), whole((C, C)), whole((HEADS, TOK, 128))]


def first_layer(x, land, gains, qkv, wvt, proj, up, down, bias):
    rows, cols, _ = x.shape
    windows = cols // WIN
    tokens = windows * TOK
    spread, pick = flag_matrices(windows, windows, False)
    land = jnp.pad(land, ((0, 0), (0, 128 - cols)))
    return pl.pallas_call(
        first_kernel,
        grid=(rows // WIN,),
        in_specs=[
            pl.BlockSpec((WIN, cols, C), lambda i: (i, 0, 0)),
            pl.BlockSpec((WIN, 128), lambda i: (i, 0)),
            *weight_specs(),
            whole(spread.shape),
            whole(pick.shape),
            whole((C, C)),
            whole((C, HID)),
            whole((HID, C)),
        ],
        out_specs=pl.BlockSpec((WIN, cols, C), lambda i: (i, 0, 0)),
        out_shape=jax.ShapeDtypeStruct((rows, cols, C), BF),
        scratch_shapes=[
            pltpu.VMEM((tokens, C), F32),
            pltpu.VMEM((tokens, C), BF),
            pltpu.VMEM((tokens, C), BF),
            pltpu.VMEM((C, tokens), BF),
            pltpu.VMEM((tokens, C), BF),
        ],
        compiler_params=pltpu.CompilerParams(vmem_limit_bytes=56 << 20),
        name="first_layer",
    )(x, land, gains, qkv, wvt, bias, jnp.asarray(spread), jnp.asarray(pick, BF), proj, up, down)


def second_layer(wide, own, land, gains, qkv, wvt, proj, up, down, bias):
    rows, cols, _ = wide.shape
    windows = cols // WIN
    tokens = (windows + 1) * TOK
    spread, pick = flag_matrices(windows + 1, windows, True)
    land = jnp.pad(land, ((0, 0), (0, 128 - cols)))
    return pl.pallas_call(
        second_kernel,
        grid=(rows // WIN,),
        in_specs=[
            pl.BlockSpec((WIN, cols, C), lambda i: (i, 0, 0)),
            pl.BlockSpec((WIN, 64, C), lambda i: (jnp.maximum(i - 1, 0), 0, 0)),
            pl.BlockSpec((WIN, 128), lambda i: (i, 0)),
            *weight_specs(),
            whole(spread.shape),
            whole(pick.shape),
            whole((C, C)),
            whole((C, HID)),
            whole((HID, C)),
        ],
        out_specs=pl.BlockSpec((WIN, 64, C), lambda i: (jnp.maximum(i - 1, 0), 0, 0)),
        out_shape=jax.ShapeDtypeStruct(own.shape, BF),
        scratch_shapes=[
            pltpu.VMEM((tokens, C), F32),
            pltpu.VMEM((tokens, C), BF),
            pltpu.VMEM((tokens, C), BF),
            pltpu.VMEM((C, tokens), BF),
            pltpu.VMEM((tokens, C), F32),
            pltpu.VMEM((WIN + SHIFT, 64, C), F32),
        ],
        compiler_params=pltpu.CompilerParams(vmem_limit_bytes=56 << 20),
        name="second_layer",
    )(wide, own, land, gains, qkv, wvt, bias, jnp.asarray(spread), jnp.asarray(pick, BF), proj, up, down)


def ring(axis, periodic):
    count = lax.axis_size(axis)
    forward = [(i, i + 1) for i in range(count - 1)]
    if periodic:
        forward.append((count - 1, 0))
    return forward, [(b, a) for a, b in forward]


def widen(block):
    forward, backward = ring("lon", True)
    left = lax.ppermute(block[:, -SHIFT:], "lon", forward)
    right = lax.ppermute(block[:, :SHIFT], "lon", backward)
    block = jnp.concatenate([block, right, left], axis=1)
    forward, backward = ring("lat", False)
    above = lax.ppermute(block[-SHIFT:], "lat", forward)
    below = lax.ppermute(block[:SHIFT], "lat", backward)
    return jnp.concatenate([above, block, below], axis=0)


def shards(fields, land, norm_gains, qkv_weight, rel_bias, proj_weight, up_weight, down_weight):
    rest = (norm_gains, qkv_weight, proj_weight, up_weight, down_weight)
    wide_land = 1 - widen(1 - land)
    settled = first_layer(fields[0], land, *layer_weights(0, *rest), bias_tiles(rel_bias[0], False))
    evolved = second_layer(widen(settled), settled, wide_land, *layer_weights(1, *rest), bias_tiles(rel_bias[1], True))
    return evolved[None]


def solution(mesh):
    return jax.shard_map(
        shards,
        mesh=mesh,
        in_specs=(P(None, "lat", "lon", None), P("lat", "lon"), P(), P(), P(), P(), P(), P()),
        out_specs=P(None, "lat", "lon", None),
        check_vma=False,
    )
```

profile of v0, /device:TPU:104, one launch (start us, length us, event | category | flops | bytes accessed | tf_op | source)
XLA Modules:
  0.0 247.1 jit_solution(9988973651199181453)
XLA Ops:
  0.8 2.2 collective-permute-start.4
  3.0 0.8 fusion.15
  3.9 1.4 fusion.16
  5.3 1.4 pad.8.land_ref
  6.7 1.9 slice_bitcast_fusion.6
  8.6 2.9 %fusion.9 = f32[24,8192]{1,0:T(8,128)S(1)} fusion(bf16[225,8192]{1,0:T(8,128)(2,1)} %constant.8.clone, bf16[12,225]{1,0:T(8,128)(2,1)S(1)} %get-tuple-element.30, bf16[12,225]{1,0:T(8,128)(2,1)S(1)} %get-tuple-element.28), kind=kOutput, calls=%fused_computation.29 | convolution fusion | flops 88495200 | bytes 4483632 | tf_op jit(solution)/shard_map/dot_general | solution.py:45
  12.5 1.6 slice_bitcast_fusion.1
  14.1 1.6 slice_bitcast_fusion
  15.7 1.6 fusion.13
  17.3 0.8 copy.25
  18.9 82.8 %first_layer.1.own_ref = bf16[64,64,384]{2,1,0:T(8,128)(2,1)} custom-call(bf16[64,64,384]{2,1,0:T(8,128)(2,1)} %bitcast.52, s32[64,128]{1,0:T(8,128)} %pad.8.land_ref, f32[2,384]{1,0:T(2,128)} %get-tuple-element.26.gain_ref, bf16[384,1152]{1,0:T(8,128)(2,1)} %get-tuple-element.14.qkv_ref, bf16[384,384]{1,0:T(8,128)(2,1)} %slice_bitcast_fusion.5.wvt_ref, ...), custom_call_target="tpu_custom_call" | custom-call | tf_op jit(solution)/shard_map/first_layer/pallas_call | solution.py:207
  101.7 2.1 fusion.12
  103.7 3.0 %collective-permute-start = (bf16[64,4,384]{2,1,0:T(4,128)(2,1)}, bf16[64,4,384]{2,1,0:T(4,128)(2,1)S(1)}, u32[]{:S(2)}, u32[]{:S(2)}) collective-permute-start(bf16[64,4,384]{2,1,0:T(4,128)(2,1)} %get-tuple-element.7), channel_id=1, source_target_pairs={{1,0},{2,1},{3,2},{4,3},{5,4},{6,5},{7,6},{0,7},{9,8},{10,9},{11,1... | collective-permute-start | bytes 589832 | tf_op jit(solution)/shard_map/ppermute | solution.py:280
  107.4 0.9 slice_add_fusion
  108.3 2.2 copy.27
  110.6 2.2 collective-permute-start.6
  112.8 3.7 %collective-permute-start.7 = (s32[4,72]{1,0:T(4,128)S(1)}, s32[4,72]{1,0:T(4,128)S(1)}, u32[]{:S(2)}, u32[]{:S(2)}) collective-permute-start(s32[4,72]{1,0:T(4,128)S(1)} %get-tuple-element.20), channel_id=1, source_target_pairs={{8,0},{16,8},{24,16},{32,24},{40,32},{48,40},{56,48},{64,56},{72,6... | collective-permute-start | bytes 3464 | tf_op jit(solution)/shard_map/ppermute | solution.py:284
  116.6 0.8 pad_maximum_fusion.3
  117.4 4.2 %collective-permute-start.2 = (bf16[4,72,384]{2,1,0:T(8,128)(2,1)S(1)}, bf16[4,72,384]{2,1,0:T(8,128)(2,1)S(1)}, u32[]{:S(2)}, u32[]{:S(2)}) collective-permute-start(bf16[4,72,384]{2,1,0:T(8,128)(2,1)S(1)} %get-tuple-element.5), channel_id=1, source_target_pairs={{0,8},{8,16},{16,24},{24,32},{32,40},{40,48},{48,56},{56,64},{64,7... | collective-permute-start | bytes 663560 | tf_op jit(solution)/shard_map/ppermute | solution.py:283
  121.6 2.1 collective-permute-start.3
  123.7 1.7 slice_bitcast_fusion.4.wvt_ref
  127.0 4.5 %collective-permute-done.3 = bf16[4,72,384]{2,1,0:T(8,128)(2,1)S(1)} collective-permute-done((bf16[4,72,384]{2,1,0:T(8,128)(2,1)S(1)}, bf16[4,72,384]{2,1,0:T(8,128)(2,1)S(1)}, u32[]{:S(2)}, u32[]{:S(2)}) %collective-permute-start.3) | collective-permute-done | bytes 221216 | tf_op jit(solution)/shard_map/ppermute | solution.py:284
  131.5 5.6 %pad_maximum_fusion.x_ref = bf16[72,72,384]{2,1,0:T(8,128)(2,1)} fusion(bf16[4,72,384]{2,1,0:T(8,128)(2,1)S(1)} %collective-permute-done.3, bf16[64,4,384]{2,1,0:T(4,128)(2,1)} %collective-permute-done.1, bf16[64,4,384]{2,1,0:T(4,128)(2,1)S(1)} %collective-permute-done, bf16[64,64,384]{2,1,0:T(8,128)(2,1)S(1)} %copy-done, ...), kind=kLoop, calls=%fused_computation | loop fusion | flops 19906560 | bytes 7962624 | tf_op jit(solution)/shard_map/concatenate | solution.py:285
  137.2 109.9 %second_layer.1 = bf16[64,64,384]{2,1,0:T(8,128)(2,1)} custom-call(bf16[72,72,384]{2,1,0:T(8,128)(2,1)} %pad_maximum_fusion.x_ref, bf16[64,64,384]{2,1,0:T(8,128)(2,1)} %first_layer.1.own_ref, s32[72,128]{1,0:T(8,128)} %pad.9.land_ref, f32[2,384]{1,0:T(2,128)} %get-tuple-element.25.gain_ref, bf16[384,1152]{1,0:T(8,128)(2,1)} %get-tuple-element.15.qkv_ref, ...), custom_call_target="tpu_custom_call" | custom-call | tf_op jit(solution)/shard_map/second_layer/pallas_call | solution.py:240
  (35 shorter events, 5.0 us)
Async XLA Ops:
  0.8 109.6 %collective-permute-start.4 = (s32[64,4]{1,0:T(8,128)S(1)}, s32[64,4]{1,0:T(8,128)S(1)}, u32[]{:S(2)}, u32[]{:S(2)}) collective-permute-start(s32[64,4]{1,0:T(8,128)S(1)} %get-tuple-element.21), channel_id=1, source_target_pairs={{1,0},{2,1},{3,2},{4,3},{5,4},{6,5},{7,6},{0,7},{9,8},{10,9},{11,1... | collective-permute-start | bytes 3080 | tf_op jit(solution)/shard_map/ppermute | solution.py:280
  3.0 107.4 %collective-permute-start.5 = (s32[64,4]{1,0:T(8,128)S(1)}, s32[64,4]{1,0:T(8,128)S(1)}, u32[]{:S(2)}, u32[]{:S(2)}) collective-permute-start(s32[64,4]{1,0:T(8,128)S(1)} %get-tuple-element.22), channel_id=1, source_target_pairs={{0,1},{1,2},{2,3},{3,4},{4,5},{5,6},{6,7},{7,0},{8,9},{9,10},{10,1... | collective-permute-start | bytes 3080 | tf_op jit(solution)/shard_map/ppermute | solution.py:279
  8.6 3.9 %copy-start.2 = (bf16[2,384,1536]{2,1,0:T(8,128)(2,1)S(1)}, bf16[2,384,1536]{2,1,0:T(8,128)(2,1)}, u32[]{:S(2)}) copy-start(bf16[2,384,1536]{2,1,0:T(8,128)(2,1)} %param.20) | copy-start | bytes 7077892
  11.5 2.5 %copy-start.3 = (bf16[2,1536,384]{2,1,0:T(8,128)(2,1)S(1)}, bf16[2,1536,384]{2,1,0:T(8,128)(2,1)}, u32[]{:S(2)}) copy-start(bf16[2,1536,384]{2,1,0:T(8,128)(2,1)} %param.21) | copy-start | bytes 7077892
  12.5 3.2 %copy-start.5 = (bf16[2,384,1152]{2,1,0:T(8,128)(2,1)S(1)}, bf16[2,384,1152]{2,1,0:T(8,128)(2,1)}, u32[]{:S(2)}) copy-start(bf16[2,384,1152]{2,1,0:T(8,128)(2,1)} %param.17) | copy-start | bytes 5308420
  18.9 87.8 %copy-start.1 = (bf16[225,8192]{1,0:T(8,128)(2,1)S(1)}, bf16[225,8192]{1,0:T(8,128)(2,1)}, u32[]{:S(2)}) copy-start(bf16[225,8192]{1,0:T(8,128)(2,1)} %constant.22.clone) | copy-start | bytes 11059204
  103.7 12.8 %collective-permute-start = (bf16[64,4,384]{2,1,0:T(4,128)(2,1)}, bf16[64,4,384]{2,1,0:T(4,128)(2,1)S(1)}, u32[]{:S(2)}, u32[]{:S(2)}) collective-permute-start(bf16[64,4,384]{2,1,0:T(4,128)(2,1)} %get-tuple-element.7), channel_id=1, source_target_pairs={{1,0},{2,1},{3,2},{4,3},{5,4},{6,5},{7,6},{0,7},{9,8},{10,9},{11,1... | collective-permute-start | bytes 589832 | tf_op jit(solution)/shard_map/ppermute | solution.py:280
  106.7 9.9 %collective-permute-start.1 = (bf16[64,4,384]{2,1,0:T(4,128)(2,1)}, bf16[64,4,384]{2,1,0:T(4,128)(2,1)}, u32[]{:S(2)}, u32[]{:S(2)}) collective-permute-start(bf16[64,4,384]{2,1,0:T(4,128)(2,1)} %get-tuple-element.8), channel_id=1, source_target_pairs={{0,1},{1,2},{2,3},{3,4},{4,5},{5,6},{6,7},{7,0},{8,9},{9,10},{10,1... | collective-permute-start | bytes 589832 | tf_op jit(solution)/shard_map/ppermute | solution.py:279
  106.7 9.9 %copy-start = (bf16[64,64,384]{2,1,0:T(8,128)(2,1)S(1)}, bf16[64,64,384]{2,1,0:T(8,128)(2,1)}, u32[]{:S(2)}) copy-start(bf16[64,64,384]{2,1,0:T(8,128)(2,1)} %first_layer.1.own_ref) | copy-start | bytes 9437188
  110.5 14.9 %copy-start.4 = (f32[12,8192]{1,0:T(8,128)S(1)}, f32[12,8192]{1,0:T(8,128)}, u32[]{:S(2)}) copy-start(f32[12,8192]{1,0:T(8,128)} %slice_add_fusion) | copy-start | bytes 1179652
  110.6 15.7 %collective-permute-start.6 = (s32[4,72]{1,0:T(4,128)S(1)}, s32[4,72]{1,0:T(4,128)S(1)}, u32[]{:S(2)}, u32[]{:S(2)}) collective-permute-start(s32[4,72]{1,0:T(4,128)S(1)} %get-tuple-element.19), channel_id=1, source_target_pairs={{0,8},{8,16},{16,24},{24,32},{32,40},{40,48},{48,56},{56,64},{64,7... | collective-permute-start | bytes 3464 | tf_op jit(solution)/shard_map/ppermute | solution.py:283
  112.8 13.5 %collective-permute-start.7 = (s32[4,72]{1,0:T(4,128)S(1)}, s32[4,72]{1,0:T(4,128)S(1)}, u32[]{:S(2)}, u32[]{:S(2)}) collective-permute-start(s32[4,72]{1,0:T(4,128)S(1)} %get-tuple-element.20), channel_id=1, source_target_pairs={{8,0},{16,8},{24,16},{32,24},{40,32},{48,40},{56,48},{64,56},{72,6... | collective-permute-start | bytes 3464 | tf_op jit(solution)/shard_map/ppermute | solution.py:284
  117.4 9.7 %collective-permute-start.2 = (bf16[4,72,384]{2,1,0:T(8,128)(2,1)S(1)}, bf16[4,72,384]{2,1,0:T(8,128)(2,1)S(1)}, u32[]{:S(2)}, u32[]{:S(2)}) collective-permute-start(bf16[4,72,384]{2,1,0:T(8,128)(2,1)S(1)} %get-tuple-element.5), channel_id=1, source_target_pairs={{0,8},{8,16},{16,24},{24,32},{32,40},{40,48},{48,56},{56,64},{64,7... | collective-permute-start | bytes 663560 | tf_op jit(solution)/shard_map/ppermute | solution.py:283
  121.6 9.9 %collective-permute-start.3 = (bf16[4,72,384]{2,1,0:T(8,128)(2,1)S(1)}, bf16[4,72,384]{2,1,0:T(8,128)(2,1)S(1)}, u32[]{:S(2)}, u32[]{:S(2)}) collective-permute-start(bf16[4,72,384]{2,1,0:T(8,128)(2,1)S(1)} %get-tuple-element.6), channel_id=1, source_target_pairs={{8,0},{16,8},{24,16},{32,24},{40,32},{48,40},{56,48},{64,56},{72,6... | collective-permute-start | bytes 663560 | tf_op jit(solution)/shard_map/ppermute | solution.py:284
where the time goes:
time: 248 us; the launch traced here: 247 us
  Pallas kernels  193 us (78%)
  local copies, waits for them, and re-layouts  20.3 us (8%)
  starting transfers between devices  17.5 us (7%)
  other arithmetic  8.3 us (3%)
  waiting for transfers between devices  4.53 us (2%)
  matrix products  3.65 us (1%)
    pallas_call x1, Pallas kernels, second_layer(): pl.pallas_call(second_kernel, grid=(rows // WIN,), in_specs=[pl.BlockSpec...  110 us
    pallas_call x1, Pallas kernels, first_layer(): pl.pallas_call(first_kernel, grid=(rows // WIN,), in_specs=[pl.BlockSpec(...  82.8 us
    ppermute x2, starting transfers between devices, widen(): above = lax.ppermute(block[-SHIFT:], 'lat', forward)  6.46 us
    ppermute x2, starting transfers between devices, widen(): below = lax.ppermute(block[:SHIFT], 'lat', backward)  5.83 us
    concatenate x1, other arithmetic, widen(): return jnp.concatenate([above, block, below], axis=0)  5.63 us
    ppermute x2, starting transfers between devices, widen(): right = lax.ppermute(block[:, :SHIFT], 'lon', backward)  5.16 us
  transfers between devices with their start and end apart: 8, of which 1 were waited for; matrix products, arithmetic and copies ran while one was open for 10% of the time, Pallas kernels for 34%

commit v1 on v0

v1 whole, which is shorter than its diff:
```python
import functools

import jax
import jax.numpy as jnp
import numpy as np
from jax import lax
from jax.experimental import pallas as pl
from jax.experimental.pallas import tpu as pltpu
from jax.sharding import PartitionSpec as P

HEADS = 12
WIN = 8
SHIFT = 4
EPS = 1e-05
C = 384
HID = 1536
TOK = WIN * WIN
BIG = 1e30
LOG2E = 1.4426950408889634
QSCALE = LOG2E / (C // HEADS) ** 0.5
BF = jnp.bfloat16
F32 = jnp.float32


WIDE = C + 128
SPAN = 2 * WIN - 1


def bias_selector(shifted):
    slot = np.arange(WIN)
    col = (slot + SHIFT) % WIN if shifted else slot
    table = np.zeros((256, WIN, 128), np.float32)
    for key in range(WIN):
        for far in range(SPAN):
            for query in range(WIN):
                table[far * SPAN + col[query] - col[key] + WIN - 1, key, far * WIN + query] = 1.0
    return table.reshape(256, WIN * 128)


def flag_matrices(windows):
    slot = np.arange(TOK) % WIN
    lane = np.arange(windows * WIN)
    spread = lane[None, :] % WIN == slot[:, None]
    pick = lane[:, None] // WIN == np.repeat(np.arange(windows), 128)[None, :]
    return spread.astype(np.float32), pick.astype(np.float32)


def normed(values, gain):
    center = jnp.mean(values, axis=-1, keepdims=True)
    moved = values - center
    spread = jnp.mean(moved * moved, axis=-1, keepdims=True)
    return (moved * lax.rsqrt(spread + EPS) * gain).astype(BF)


def dot_nt(a, b):
    return lax.dot_general(a, b, (((1,), (1,)), ((), ())), preferred_element_type=F32)


def dot_nn(a, b):
    return jnp.dot(a, b, preferred_element_type=F32)


def score_pair(qt_ref, k_ref, bias_ref, s_ref, mask, pair):
    here = pl.ds(pair * 128, 128)
    first = lax.broadcasted_iota(jnp.int32, (TOK, 128), 1) < TOK
    zero = jnp.zeros((32, 128), BF)
    for group in range(3):
        keys = k_ref[here, pl.ds(group * 128, 128)]
        for half in range(2):
            base = group * 4 + 2 * half
            columns = []
            for j in range(2):
                blocks = [zero] * 4
                blocks[2 * half + j] = qt_ref[pl.ds((base + j) * 32, 32), here]
                columns.append(jnp.concatenate(blocks, axis=0))
            scores = dot_nn(keys, jnp.concatenate(columns, axis=1))
            for j in range(2):
                both = scores[:, j * 128 : (j + 1) * 128]
                s_ref[pair % 2, base + j] = jnp.where(first, both[:TOK], both[TOK:]) + (bias_ref[base + j] + mask)


def weigh_pair(s_ref, p_ref, pair):
    side = lax.broadcasted_iota(jnp.int32, (1, 128), 1) < TOK
    for head in range(HEADS):
        s = s_ref[pair % 2, head]
        e = jnp.exp2(s - jnp.max(s, axis=0, keepdims=True))
        inv = 1.0 / jnp.sum(e, axis=0, keepdims=True)
        lanes = pl.ds(head % 2 * 128, 128)
        p_ref[pair % 2, head // 2, :TOK, lanes] = (e * jnp.where(side, inv, 0.0)).astype(BF)
        p_ref[pair % 2, head // 2, TOK:, lanes] = (e * jnp.where(side, 0.0, inv)).astype(BF)


def mix_pair(vt_ref, p_ref, ot_ref, pair):
    here = pl.ds(pair * 128, 128)
    for two in range(HEADS // 2):
        mixed = dot_nn(vt_ref[pl.ds(two * 64, 64), here], p_ref[pair % 2, two])
        ot_ref[pl.ds(two * 64, 32), here] = mixed[:32, :128]
        ot_ref[pl.ds(two * 64 + 32, 32), here] = mixed[32:, 128:]


def attend(qt_ref, k_ref, vt_ref, bias_ref, s_ref, p_ref, ot_ref, ocean, pairs):
    key = lax.broadcasted_iota(jnp.int32, (TOK, 128), 0)
    lane = lax.broadcasted_iota(jnp.int32, (TOK, 128), 1)

    def score(pair):
        flags = jnp.where(lane < TOK, ocean(2 * pair), ocean(2 * pair + 1))
        mask = jnp.where((lane % TOK == key) | (flags > 0.5), 0.0, -BIG)
        score_pair(qt_ref, k_ref, bias_ref, s_ref, mask, pair)

    score(0)
    for pair in range(pairs):
        if pair + 1 < pairs:
            score(pair + 1)
        weigh_pair(s_ref, p_ref, pair)
        mix_pair(vt_ref, p_ref, ot_ref, pair)


def finish(x, mixed, proj_ref, gain, up_ref, down_ref):
    mid = (x + dot_nn(mixed, proj_ref[...])).astype(BF).astype(F32)
    hidden = dot_nn(normed(mid, gain), up_ref[...])
    hidden = jax.nn.gelu(hidden, approximate=True).astype(BF)
    return mid + dot_nn(hidden, down_ref[...])


def project(x_win, gain, qkv_ref, wt_ref, qt_ref, k_ref, vt_ref):
    packed = normed(x_win, gain)
    qt_ref[...] = (dot_nt(wt_ref[:C], packed) * QSCALE).astype(BF)
    k_ref[...] = dot_nn(packed, qkv_ref[:, C : 2 * C]).astype(BF)
    vt_ref[...] = dot_nt(wt_ref[C:], packed).astype(BF)


def prepare(qkv_ref, table_ref, select_ref, wt_ref, tab_ref, row_ref, bias_ref):
    @pl.when(pl.program_id(0) == 0)
    def _():
        wt_ref[:C] = qkv_ref[:, :C].T
        wt_ref[C:] = qkv_ref[:, 2 * C :].T
        tab_ref[...] = jnp.zeros_like(tab_ref)
        tab_ref[:HEADS, : SPAN * SPAN] = table_ref[...] * LOG2E
        high = tab_ref[...].astype(BF)
        low = (tab_ref[...] - high.astype(F32)).astype(BF)
        picked = dot_nn(high, select_ref[...]) + dot_nn(low, select_ref[...])
        for key in range(WIN):
            for head in range(HEADS):
                row_ref[head, key : key + 1] = picked[head : head + 1, key * 128 : (key + 1) * 128]
        first = lax.broadcasted_iota(jnp.int32, (WIN, 128), 1) < TOK
        for head in range(HEADS):
            rows = row_ref[head]
            for row in range(WIN):
                back = (WIN - 1 - row) * WIN
                left = pltpu.roll(rows, (128 - back) % 128, 1)
                right = pltpu.roll(rows, (TOK - back) % 128, 1)
                bias_ref[head, row * WIN : (row + 1) * WIN] = jnp.where(first, left, right)


def first_kernel(x_ref, land_ref, gain_ref, qkv_ref, table_ref, select_ref, proj_ref, up_ref, down_ref, spread_ref, pick_ref,
                 out_ref, wt_ref, tab_ref, row_ref, bias_ref, xw_ref, qt_ref, k_ref, vt_ref, s_ref, p_ref, ot_ref, o_ref):
    windows = 8
    prepare(qkv_ref, table_ref, select_ref, wt_ref, tab_ref, row_ref, bias_ref)
    for r in range(WIN):
        for w in range(windows):
            xw_ref[pl.ds(w * TOK + r * WIN, WIN), :] = x_ref[0, r, pl.ds(w * WIN, WIN), :].astype(F32)
    project(xw_ref[...], gain_ref[0:1], qkv_ref, wt_ref, qt_ref, k_ref, vt_ref)
    flags = (1 - land_ref[...]).astype(F32)
    rows = jnp.broadcast_to(flags[:, None, :], (WIN, WIN, windows * WIN)).reshape(TOK, windows * WIN)
    ocean = dot_nn((rows * spread_ref[...]).astype(BF), pick_ref[...])
    attend(qt_ref, k_ref, vt_ref, bias_ref, s_ref, p_ref, ot_ref, lambda w: ocean[:, w * 128 : (w + 1) * 128], windows // 2)
    o_ref[...] = ot_ref[...].astype(BF).T
    result = finish(xw_ref[...], o_ref[...], proj_ref, gain_ref[1:2], up_ref, down_ref)
    for r in range(WIN):
        for w in range(windows):
            out_ref[r, pl.ds(w * WIN, WIN), :C] = result[w * TOK + r * WIN : w * TOK + (r + 1) * WIN].astype(BF)
            out_ref[r, pl.ds(w * WIN, WIN), C:] = ocean[r * WIN : (r + 1) * WIN, w * 128 : (w + 1) * 128].astype(BF)


def second_kernel(low_ref, high_ref, low_side_ref, high_side_ref, above_ref, below_ref, own_ref,
                  gain_ref, qkv_ref, table_ref, select_ref, proj_ref, up_ref, down_ref,
                  out_ref, wt_ref, tab_ref, row_ref, bias_ref, xw_ref, qt_ref, k_ref, vt_ref, s_ref, p_ref, ot_ref, o_ref, att_ref):
    windows = 9
    step = pl.program_id(0)
    last = step == pl.num_programs(0) - 1
    prepare(qkv_ref, table_ref, select_ref, wt_ref, tab_ref, row_ref, bias_ref)
    low = lax.broadcasted_iota(jnp.int32, (WIN, C), 0) < SHIFT
    low_wide = lax.broadcasted_iota(jnp.int32, (WIN, WIDE), 0) < SHIFT
    for r in range(WIN):
        near, side, far, edge = (low_ref, low_side_ref, above_ref, step == 0) if r < SHIFT else (high_ref, high_side_ref, below_ref, last)
        tiles = []
        for t in range(windows):
            inner = near[r % SHIFT, pl.ds(t * WIN, WIN), :] if t < 8 else side[r % SHIFT]
            tiles.append(jnp.where(edge, far[r % SHIFT, pl.ds(t * WIN, WIN), :].astype(F32), inner.astype(F32)))
        for w in range(windows):
            xw_ref[pl.ds(w * TOK + r * WIN, WIN), :] = jnp.where(low_wide, tiles[w], tiles[(w - 1) % windows])
    xw_ref[pl.ds(windows * TOK, TOK), :] = jnp.zeros((TOK, WIDE), F32)
    project(xw_ref[:, :C], gain_ref[2:3], qkv_ref, wt_ref, qt_ref, k_ref, vt_ref)
    attend(qt_ref, k_ref, vt_ref, bias_ref, s_ref, p_ref, ot_ref, lambda w: xw_ref[pl.ds(w * TOK, TOK), C:], 5)
    o_ref[...] = ot_ref[...].T
    for t in range(8):
        for r in range(WIN):
            left = o_ref[pl.ds(t * TOK + r * WIN, WIN), :]
            right = o_ref[pl.ds((t + 1) * TOK + r * WIN, WIN), :]
            att_ref[r + SHIFT, pl.ds(t * WIN, WIN), :] = jnp.where(low, left, right)

    @pl.when(step > 0)
    def _():
        mixed = att_ref[0:WIN].reshape(WIN * 64, C).astype(BF)
        x = own_ref[...].astype(F32).reshape(WIN * 64, C)
        result = finish(x, mixed, proj_ref, gain_ref[3:4], up_ref, down_ref)
        out_ref[0] = result.reshape(WIN, 64, C).astype(BF)

    att_ref[0:SHIFT] = att_ref[WIN : WIN + SHIFT]


def whole(*shape):
    return pl.BlockSpec(shape, lambda i: (0,) * len(shape), pipeline_mode=pl.Buffered(1))


def of_layer(layer, *shape):
    return pl.BlockSpec((None, *shape), lambda i: (layer, 0, 0), pipeline_mode=pl.Buffered(1))


def weight_specs(layer):
    return [
        whole(4, C),
        of_layer(layer, C, 3 * C),
        of_layer(layer, HEADS, SPAN * SPAN),
        whole(256, WIN * 128),
        of_layer(layer, C, C),
        of_layer(layer, C, HID),
        of_layer(layer, HID, C),
    ]


def scratch(tokens, width):
    return [
        pltpu.VMEM((2 * C, C), BF),
        pltpu.VMEM((16, 256), F32),
        pltpu.VMEM((HEADS, WIN, 128), F32),
        pltpu.VMEM((HEADS, TOK, 128), F32),
        pltpu.VMEM((tokens, width), F32),
        pltpu.VMEM((C, tokens), BF),
        pltpu.VMEM((tokens, C), BF),
        pltpu.VMEM((C, tokens), BF),
        pltpu.VMEM((2, HEADS, TOK, 128), F32),
        pltpu.VMEM((2, HEADS // 2, 128, 256), BF),
        pltpu.VMEM((C, tokens), F32),
    ]


PARAMS = pltpu.CompilerParams(vmem_limit_bytes=56 << 20)


def first_layer(fields, land, weights):
    _, rows, cols, _ = fields.shape
    windows = cols // WIN
    tokens = windows * TOK
    spread, pick = flag_matrices(windows)
    return pl.pallas_call(
        first_kernel,
        grid=(rows // WIN,),
        in_specs=[
            pl.BlockSpec((1, WIN, cols, C), lambda i: (0, i, 0, 0)),
            pl.BlockSpec((WIN, cols), lambda i: (i, 0)),
            *weight_specs(0),
            whole(*spread.shape),
            whole(*pick.shape),
        ],
        out_specs=pl.BlockSpec((WIN, cols, WIDE), lambda i: (i, 0, 0)),
        out_shape=jax.ShapeDtypeStruct((rows, cols, WIDE), BF),
        scratch_shapes=[*scratch(tokens, C), pltpu.VMEM((tokens, C), BF)],
        compiler_params=PARAMS,
        name="first_layer",
    )(fields, land, *weights(False), jnp.asarray(spread), jnp.asarray(pick, BF))


def second_layer(own, side, above, below, weights):
    rows, cols, _ = own.shape
    bands = rows // WIN
    tokens = (cols // WIN + 2) * TOK
    lower = lambda i: (jnp.maximum(2 * i - 1, 0), 0, 0)
    upper = lambda i: (jnp.minimum(2 * i, 2 * bands - 1), 0, 0)
    done = lambda i: jnp.maximum(i - 1, 0)
    return pl.pallas_call(
        second_kernel,
        grid=(bands + 1,),
        in_specs=[
            pl.BlockSpec((SHIFT, cols, WIDE), lower),
            pl.BlockSpec((SHIFT, cols, WIDE), upper),
            pl.BlockSpec((SHIFT, WIN, WIDE), lower),
            pl.BlockSpec((SHIFT, WIN, WIDE), upper),
            whole(SHIFT, cols + WIN, WIDE),
            whole(SHIFT, cols + WIN, WIDE),
            pl.BlockSpec((WIN, cols, C), lambda i: (done(i), 0, 0)),
            *weight_specs(1),
        ],
        out_specs=pl.BlockSpec((1, WIN, cols, C), lambda i: (0, done(i), 0, 0)),
        out_shape=jax.ShapeDtypeStruct((1, rows, cols, C), BF),
        scratch_shapes=[*scratch(tokens, WIDE), pltpu.VMEM((tokens, C), F32), pltpu.VMEM((WIN + SHIFT, cols, C), F32)],
        compiler_params=PARAMS,
        name="second_layer",
    )(own, own, side, side, above, below, own, *weights(True))


def ring(axis, periodic):
    count = lax.axis_size(axis)
    forward = [(i, i + 1) for i in range(count - 1)]
    if periodic:
        forward.append((count - 1, 0))
    return forward, [(b, a) for a, b in forward]


def borders(block):
    forward, backward = ring("lon", True)
    left = lax.ppermute(block[:, -SHIFT:], "lon", forward)
    right = lax.ppermute(block[:, :SHIFT], "lon", backward)
    side = jnp.concatenate([right, left], axis=1)
    forward, backward = ring("lat", False)
    above = lax.ppermute(jnp.concatenate([block[-SHIFT:], side[-SHIFT:]], axis=1), "lat", forward)
    below = lax.ppermute(jnp.concatenate([block[:SHIFT], side[:SHIFT]], axis=1), "lat", backward)
    return side, above, below


def shards(fields, land, norm_gains, qkv_weight, rel_bias, proj_weight, up_weight, down_weight):
    def weights(shifted):
        return (norm_gains, qkv_weight, rel_bias, jnp.asarray(bias_selector(shifted), BF), proj_weight, up_weight, down_weight)

    settled = first_layer(fields, land, weights)
    return second_layer(settled, *borders(settled), weights)


def solution(mesh):
    return jax.shard_map(
        shards,
        mesh=mesh,
        in_specs=(P(None, "lat", "lon", None), P("lat", "lon"), P(), P(), P(), P(), P(), P()),
        out_specs=P(None, "lat", "lon", None),
        check_vma=False,
    )
```

time: 248 us -> 117 us (0.47)
  Pallas kernels: 193 us -> 90.8 us
  local copies, waits for them, and re-layouts: 20.3 us -> 4.53 us
  starting transfers between devices: 17.5 us -> 8.05 us
  waiting for transfers between devices: 4.53 us -> 11.9 us
  other arithmetic: 8.3 us -> 1.15 us
  matrix products: 3.65 us -> 0 us
    pallas_call x1, Pallas kernels: 110 us -> 49.6 us  [second_layer(): pl.pallas_call(second_kernel, grid=(bands + 1,), in_specs=[pl.BlockSpec((...]
    pallas_call x1, Pallas kernels: 82.8 us -> 41.2 us  [first_layer(): pl.pallas_call(first_kernel, grid=(rows // WIN,), in_specs=[pl.BlockSpec(...]
    ppermute x8 -> x4, starting transfers between devices: 17.5 us -> 8.05 us  [the longest x1 3.72 us: borders(): lax.ppermute(jnp.concatenate([block[:SHIFT], side[:SHIFT]], axis=1), 'lat...]
    ppermute x8 -> x4, waiting for transfers between devices: 4.53 us -> 11.9 us  [the longest x1 4.27 us: borders(): lax.ppermute(jnp.concatenate([block[:SHIFT], side[:SHIFT]], axis=1), 'lat...]
    squeeze x3 -> x0, local copies, waits for them, and re-layouts: 5.11 us -> none  [the longest x1 1.92 us: layer_weights(): proj_weight[layer]]
    concatenate x1 -> x4, other arithmetic: 5.63 us -> 1.15 us  [the longest x2 1.11 us: borders(): side = jnp.concatenate([right, left], axis=1)]
    dot_general x2 -> x0, matrix products: 3.65 us -> none  [bias_tiles(): jnp.dot(both, jnp.asarray(bias_selector(shifted), BF), preferred_element_...]
    slice x5 -> x2, local copies, waits for them, and re-layouts: 5.93 us -> 2.47 us  [the longest x1 1.41 us: borders(): right = lax.ppermute(block[:, :SHIFT], 'lon', backward)]
  transfers between devices with their start and end apart: 8 -> 4, of which waited for: 1 -> 4; matrix products, arithmetic and copies ran while one was open for 10% -> 2% of each run, Pallas kernels for 34% -> 0%
where the time goes in v1:
time: 117 us; the launch traced here: 116 us
  Pallas kernels  90.8 us (78%)
  waiting for transfers between devices  11.9 us (10%)
  starting transfers between devices  8.05 us (7%)
  local copies, waits for them, and re-layouts  4.53 us (4%)
    pallas_call x1, Pallas kernels, second_layer(): pl.pallas_call(second_kernel, grid=(bands + 1,), in_specs=[pl.BlockSpec((...  49.6 us
    pallas_call x1, Pallas kernels, first_layer(): pl.pallas_call(first_kernel, grid=(rows // WIN,), in_specs=[pl.BlockSpec(...  41.2 us
    ppermute x1, waiting for transfers between devices, borders(): lax.ppermute(jnp.concatenate([block[:SHIFT], side[:SHIFT]], axis=1), 'lat...  4.27 us
    ppermute x1, starting transfers between devices, borders(): lax.ppermute(jnp.concatenate([block[:SHIFT], side[:SHIFT]], axis=1), 'lat...  3.72 us
    ppermute x1, waiting for transfers between devices, borders(): left = lax.ppermute(block[:, -SHIFT:], 'lon', forward)  3.12 us
    ppermute x1, waiting for transfers between devices, borders(): right = lax.ppermute(block[:, :SHIFT], 'lon', backward)  2.82 us
  transfers between devices with their start and end apart: 4, of which 4 were waited for; matrix products, arithmetic and copies ran while one was open for 2% of the time, Pallas kernels for 0%

profile of v1, /device:TPU:104, one launch (start us, length us, event | category | flops | bytes accessed | tf_op | source)
XLA Modules:
  0.0 116.5 jit_solution(1043663580930296990)
XLA Ops:
  0.0 1.4 %copy.13.table_ref = f32[2,12,225]{2,1,0:T(8,128)} copy(f32[2,12,225]{2,0,1:T(2,128)} %param.16) | data formatting | bytes 43200 | tf_op args[4]
  1.4 41.2 %first_layer.1.low_ref.high_ref.own_ref = bf16[64,64,512]{2,1,0:T(8,128)(2,1)} custom-call(bf16[1,64,64,384]{3,2,1,0:T(8,128)(2,1)} %x_ref.1, s32[64,64]{1,0:T(8,128)} %land_ref.1, f32[4,384]{1,0:T(4,128)} %gain_ref.3, bf16[2,384,1152]{2,1,0:T(8,128)(2,1)} %qkv_ref.3, f32[2,12,225]{2,1,0:T(8,128)} %copy.13.table_ref, ...), custom_call_target="tpu_custom_call" | custom-call | tf_op jit(solution)/shard_map/first_layer/pallas_call | solution.py:256
  42.6 1.4 %fusion.3 = (bf16[64,4,512]{2,1,0:T(4,128)(2,1)S(1)}, bf16[64,4,512]{2,1,0:T(4,128)(2,1)S(1)}) fusion(bf16[64,64,512]{2,1,0:T(8,128)(2,1)} %first_layer.1.low_ref.high_ref.own_ref), kind=kLoop, calls=%fused_computation.10 | loop fusion | bytes 1048576 | tf_op jit(solution)/shard_map/slice | solution.py:313
  44.0 2.2 %collective-permute-start = (bf16[64,4,512]{2,1,0:T(4,128)(2,1)S(1)}, bf16[64,4,512]{2,1,0:T(4,128)(2,1)S(1)}, u32[]{:S(2)}, u32[]{:S(2)}) collective-permute-start(bf16[64,4,512]{2,1,0:T(4,128)(2,1)S(1)} %get-tuple-element.7), channel_id=1, source_target_pairs={{1,0},{2,1},{3,2},{4,3},{5,4},{6,5},{7,6},{0,7},{9,8},{10,9},{11,1... | collective-permute-start | bytes 786440 | tf_op jit(solution)/shard_map/ppermute | solution.py:313
  46.2 0.0 collective-permute-start.1
  46.2 1.1 fusion.2
  47.2 2.8 %collective-permute-done = bf16[64,4,512]{2,1,0:T(4,128)(2,1)S(1)} collective-permute-done((bf16[64,4,512]{2,1,0:T(4,128)(2,1)S(1)}, bf16[64,4,512]{2,1,0:T(4,128)(2,1)S(1)}, u32[]{:S(2)}, u32[]{:S(2)}) %collective-permute-start) | collective-permute-done | bytes 262176 | tf_op jit(solution)/shard_map/ppermute | solution.py:313
  50.1 3.1 %collective-permute-done.1 = bf16[64,4,512]{2,1,0:T(4,128)(2,1)S(1)} collective-permute-done((bf16[64,4,512]{2,1,0:T(4,128)(2,1)S(1)}, bf16[64,4,512]{2,1,0:T(4,128)(2,1)S(1)}, u32[]{:S(2)}, u32[]{:S(2)}) %collective-permute-start.1) | collective-permute-done | bytes 262176 | tf_op jit(solution)/shard_map/ppermute | solution.py:312
  53.2 2.1 %collective-permute-start.2 = (bf16[4,72,512]{2,1,0:T(8,128)(2,1)S(1)}, bf16[4,72,512]{2,1,0:T(8,128)(2,1)S(1)}, u32[]{:S(2)}, u32[]{:S(2)}) collective-permute-start(bf16[4,72,512]{2,1,0:T(8,128)(2,1)S(1)} %pad_maximum_fusion.1), channel_id=1, source_target_pairs={{0,8},{8,16},{16,24},{24,32},{32,40},{40,48},{48,56},{56,64},{64,7... | collective-permute-start | bytes 884744 | tf_op jit(solution)/shard_map/ppermute | solution.py:316
  55.4 3.7 %collective-permute-start.3 = (bf16[4,72,512]{2,1,0:T(8,128)(2,1)S(1)}, bf16[4,72,512]{2,1,0:T(8,128)(2,1)S(1)}, u32[]{:S(2)}, u32[]{:S(2)}) collective-permute-start(bf16[4,72,512]{2,1,0:T(8,128)(2,1)S(1)} %pad_maximum_fusion.2), channel_id=1, source_target_pairs={{8,0},{16,8},{24,16},{32,24},{40,32},{48,40},{56,48},{64,56},{72,6... | collective-permute-start | bytes 884744 | tf_op jit(solution)/shard_map/ppermute | solution.py:317
  59.1 1.1 pad_maximum_fusion.low_side_ref.high_side_ref
  60.2 1.7 %collective-permute-done.2.above_ref = bf16[4,72,512]{2,1,0:T(8,128)(2,1)S(1)} collective-permute-done((bf16[4,72,512]{2,1,0:T(8,128)(2,1)S(1)}, bf16[4,72,512]{2,1,0:T(8,128)(2,1)S(1)}, u32[]{:S(2)}, u32[]{:S(2)}) %collective-permute-start.2) | collective-permute-done | bytes 294944 | tf_op jit(solution)/shard_map/ppermute | solution.py:316
  61.9 0.0 copy-start
  61.9 4.3 %collective-permute-done.3.below_ref = bf16[4,72,512]{2,1,0:T(8,128)(2,1)S(1)} collective-permute-done((bf16[4,72,512]{2,1,0:T(8,128)(2,1)S(1)}, bf16[4,72,512]{2,1,0:T(8,128)(2,1)S(1)}, u32[]{:S(2)}, u32[]{:S(2)}) %collective-permute-start.3) | collective-permute-done | bytes 294944 | tf_op jit(solution)/shard_map/ppermute | solution.py:317
  66.1 0.0 copy-done
  66.1 0.0 copy-start.1
  66.1 0.7 copy-done.1
  66.8 49.6 %second_layer.1 = bf16[1,64,64,384]{3,2,1,0:T(8,128)(2,1)} custom-call(bf16[64,64,512]{2,1,0:T(8,128)(2,1)} %first_layer.1.low_ref.high_ref.own_ref, bf16[64,64,512]{2,1,0:T(8,128)(2,1)} %first_layer.1.low_ref.high_ref.own_ref, bf16[64,8,512]{2,1,0:T(8,128)(2,1)} %pad_maximum_fusion.low_side_ref.high_side_ref, ...), custom_call_target="tpu_custom_call" | custom-call | tf_op jit(solution)/shard_map/second_layer/pallas_call | solution.py:281
  (3 shorter events, 0.1 us)
Async XLA Ops:
  44.0 6.1 %collective-permute-start = (bf16[64,4,512]{2,1,0:T(4,128)(2,1)S(1)}, bf16[64,4,512]{2,1,0:T(4,128)(2,1)S(1)}, u32[]{:S(2)}, u32[]{:S(2)}) collective-permute-start(bf16[64,4,512]{2,1,0:T(4,128)(2,1)S(1)} %get-tuple-element.7), channel_id=1, source_target_pairs={{1,0},{2,1},{3,2},{4,3},{5,4},{6,5},{7,6},{0,7},{9,8},{10,9},{11,1... | collective-permute-start | bytes 786440 | tf_op jit(solution)/shard_map/ppermute | solution.py:313
  46.2 7.0 %collective-permute-start.1 = (bf16[64,4,512]{2,1,0:T(4,128)(2,1)S(1)}, bf16[64,4,512]{2,1,0:T(4,128)(2,1)S(1)}, u32[]{:S(2)}, u32[]{:S(2)}) collective-permute-start(bf16[64,4,512]{2,1,0:T(4,128)(2,1)S(1)} %get-tuple-element.8), channel_id=1, source_target_pairs={{0,1},{1,2},{2,3},{3,4},{4,5},{5,6},{6,7},{7,0},{8,9},{9,10},{10,1... | collective-permute-start | bytes 786440 | tf_op jit(solution)/shard_map/ppermute | solution.py:312
  53.2 8.6 %collective-permute-start.2 = (bf16[4,72,512]{2,1,0:T(8,128)(2,1)S(1)}, bf16[4,72,512]{2,1,0:T(8,128)(2,1)S(1)}, u32[]{:S(2)}, u32[]{:S(2)}) collective-permute-start(bf16[4,72,512]{2,1,0:T(8,128)(2,1)S(1)} %pad_maximum_fusion.1), channel_id=1, source_target_pairs={{0,8},{8,16},{16,24},{24,32},{32,40},{40,48},{48,56},{56,64},{64,7... | collective-permute-start | bytes 884744 | tf_op jit(solution)/shard_map/ppermute | solution.py:316
  55.4 10.7 %collective-permute-start.3 = (bf16[4,72,512]{2,1,0:T(8,128)(2,1)S(1)}, bf16[4,72,512]{2,1,0:T(8,128)(2,1)S(1)}, u32[]{:S(2)}, u32[]{:S(2)}) collective-permute-start(bf16[4,72,512]{2,1,0:T(8,128)(2,1)S(1)} %pad_maximum_fusion.2), channel_id=1, source_target_pairs={{8,0},{16,8},{24,16},{32,24},{40,32},{48,40},{56,48},{64,56},{72,6... | collective-permute-start | bytes 884744 | tf_op jit(solution)/shard_map/ppermute | solution.py:317
  61.9 4.3 %copy-start = (bf16[4,72,512]{2,1,0:T(8,128)(2,1)}, bf16[4,72,512]{2,1,0:T(8,128)(2,1)S(1)}, u32[]{:S(2)}) copy-start(bf16[4,72,512]{2,1,0:T(8,128)(2,1)S(1)} %collective-permute-done.2.above_ref) | copy-start | bytes 884740
  66.1 0.7 copy-start.1

commit v2 on v1

--- a/solution.py
+++ b/solution.py
@@ -19,6 +19,9 @@
 LOG2E = 1.4426950408889634
 QSCALE = LOG2E / (C // HEADS) ** 0.5
 BF = jnp.bfloat16
+UP_CHUNK = 256
+ORDER_FIRST = "abaabaabababaababaabaab"
+ORDER_SECOND = "abaaabaaabaaabaaabaaabab"
 F32 = jnp.float32
 
 
@@ -98,7 +101,7 @@
         ot_ref[pl.ds(two * 64 + 32, 32), here] = mixed[32:, 128:]
 
 
-def attend(qt_ref, k_ref, vt_ref, bias_ref, s_ref, p_ref, ot_ref, ocean, pairs):
+def attend_stages(qt_ref, k_ref, vt_ref, bias_ref, s_ref, p_ref, ot_ref, ocean, pairs):
     key = lax.broadcasted_iota(jnp.int32, (TOK, 128), 0)
     lane = lax.broadcasted_iota(jnp.int32, (TOK, 128), 1)
 
@@ -107,19 +110,45 @@
         mask = jnp.where((lane % TOK == key) | (flags > 0.5), 0.0, -BIG)
         score_pair(qt_ref, k_ref, bias_ref, s_ref, mask, pair)
 
-    score(0)
+    stages = [lambda: score(0)]
     for pair in range(pairs):
         if pair + 1 < pairs:
-            score(pair + 1)
-        weigh_pair(s_ref, p_ref, pair)
-        mix_pair(vt_ref, p_ref, ot_ref, pair)
-
-
-def finish(x, mixed, proj_ref, gain, up_ref, down_ref):
-    mid = (x + dot_nn(mixed, proj_ref[...])).astype(BF).astype(F32)
-    hidden = dot_nn(normed(mid, gain), up_ref[...])
-    hidden = jax.nn.gelu(hidden, approximate=True).astype(BF)
-    return mid + dot_nn(hidden, down_ref[...])
+            stages.append(lambda pair=pair: score(pair + 1))
+        stages.append(lambda pair=pair: weigh_pair(s_ref, p_ref, pair))
+        stages.append(lambda pair=pair: mix_pair(vt_ref, p_ref, ot_ref, pair))
+    return stages
+
+
+def finish_stages(x_tile, mixed_ref, mid_ref, n_ref, hid_ref, proj_ref, gain, up_ref, down_ref, store):
+    def head():
+        for tile in range(8):
+            for r in range(WIN):
+                mid_ref[pl.ds(tile * TOK + r * WIN, WIN), :] = x_tile(r, tile).astype(F32)
+        mid = (mid_ref[...] + dot_nn(mixed_ref[...], proj_ref[...])).astype(BF).astype(F32)
+        mid_ref[...] = mid
+        n_ref[...] = normed(mid, gain)
+
+    def up(at):
+        lanes = pl.ds(at, UP_CHUNK)
+        hid_ref[:, lanes] = jax.nn.gelu(dot_nn(n_ref[...], up_ref[:, lanes]), approximate=True).astype(BF)
+
+    def down():
+        result = mid_ref[...] + dot_nn(hid_ref[...], down_ref[...])
+        for tile in range(8):
+            for r in range(WIN):
+                store(r, tile, result[tile * TOK + r * WIN : tile * TOK + (r + 1) * WIN].astype(BF))
+
+    return [head] + [functools.partial(up, at) for at in range(0, HID, UP_CHUNK)] + [down]
+
+
+def run(order, first, second):
+    first, second = list(first), list(second)
+    for which in order:
+        stages = first if which == "a" else second
+        if stages:
+            stages.pop(0)()
+    for stage in first + second:
+        stage()
 
 
 def project(x_win, gain, qkv_ref, wt_ref, qt_ref, k_ref, vt_ref):
@@ -130,83 +159,131 @@
 
 
 def prepare(qkv_ref, table_ref, select_ref, wt_ref, tab_ref, row_ref, bias_ref):
-    @pl.when(pl.program_id(0) == 0)
-    def _():
-        wt_ref[:C] = qkv_ref[:, :C].T
-        wt_ref[C:] = qkv_ref[:, 2 * C :].T
-        tab_ref[...] = jnp.zeros_like(tab_ref)
-        tab_ref[:HEADS, : SPAN * SPAN] = table_ref[...] * LOG2E
-        high = tab_ref[...].astype(BF)
-        low = (tab_ref[...] - high.astype(F32)).astype(BF)
-        picked = dot_nn(high, select_ref[...]) + dot_nn(low, select_ref[...])
-        for key in range(WIN):
-            for head in range(HEADS):
-                row_ref[head, key : key + 1] = picked[head : head + 1, key * 128 : (key + 1) * 128]
-        first = lax.broadcasted_iota(jnp.int32, (WIN, 128), 1) < TOK
+    wt_ref[:C] = qkv_ref[:, :C].T
+    wt_ref[C:] = qkv_ref[:, 2 * C :].T
+    tab_ref[...] = jnp.zeros_like(tab_ref)
+    tab_ref[:HEADS, : SPAN * SPAN] = table_ref[...] * LOG2E
+    high = tab_ref[...].astype(BF)
+    low = (tab_ref[...] - high.astype(F32)).astype(BF)
+    picked = dot_nn(high, select_ref[...]) + dot_nn(low, select_ref[...])
+    for key in range(WIN):
         for head in range(HEADS):
-            rows = row_ref[head]
-            for row in range(WIN):
-                back = (WIN - 1 - row) * WIN
-                left = pltpu.roll(rows, (128 - back) % 128, 1)
-                right = pltpu.roll(rows, (TOK - back) % 128, 1)
-                bias_ref[head, row * WIN : (row + 1) * WIN] = jnp.where(first, left, right)
-
-
-def first_kernel(x_ref, land_ref, gain_ref, qkv_ref, table_ref, select_ref, proj_ref, up_ref, down_ref, spread_ref, pick_ref,
-                 out_ref, wt_ref, tab_ref, row_ref, bias_ref, xw_ref, qt_ref, k_ref, vt_ref, s_ref, p_ref, ot_ref, o_ref):
+            row_ref[head, key : key + 1] = picked[head : head + 1, key * 128 : (key + 1) * 128]
+    first = lax.broadcasted_iota(jnp.int32, (WIN, 128), 1) < TOK
+    for head in range(HEADS):
+        rows = row_ref[head]
+        for row in range(WIN):
+            back = (WIN - 1 - row) * WIN
+            left = pltpu.roll(rows, (128 - back) % 128, 1)
+            right = pltpu.roll(rows, (TOK - back) % 128, 1)
+            bias_ref[head, row * WIN : (row + 1) * WIN] = jnp.where(first, left, right)
+
+
+def first_kernel(x_ref, before_ref, land_ref, gain_ref, qkv_ref, table_ref, select_ref, proj_ref, up_ref, down_ref, spread_ref, pick_ref,
+                 out_ref, wt_ref, tab_ref, row_ref, bias_ref, xw_ref, qt_ref, k_ref, vt_ref, s_ref, p_ref, ot_ref,
+                 mixed_ref, mid_ref, n_ref, hid_ref, ocean_ref, flag_ref):
     windows = 8
-    prepare(qkv_ref, table_ref, select_ref, wt_ref, tab_ref, row_ref, bias_ref)
-    for r in range(WIN):
-        for w in range(windows):
-            xw_ref[pl.ds(w * TOK + r * WIN, WIN), :] = x_ref[0, r, pl.ds(w * WIN, WIN), :].astype(F32)
-    project(xw_ref[...], gain_ref[0:1], qkv_ref, wt_ref, qt_ref, k_ref, vt_ref)
-    flags = (1 - land_ref[...]).astype(F32)
-    rows = jnp.broadcast_to(flags[:, None, :], (WIN, WIN, windows * WIN)).reshape(TOK, windows * WIN)
-    ocean = dot_nn((rows * spread_ref[...]).astype(BF), pick_ref[...])
-    attend(qt_ref, k_ref, vt_ref, bias_ref, s_ref, p_ref, ot_ref, lambda w: ocean[:, w * 128 : (w + 1) * 128], windows // 2)
-    o_ref[...] = ot_ref[...].astype(BF).T
-    result = finish(xw_ref[...], o_ref[...], proj_ref, gain_ref[1:2], up_ref, down_ref)
-    for r in range(WIN):
-        for w in range(windows):
-            out_ref[r, pl.ds(w * WIN, WIN), :C] = result[w * TOK + r * WIN : w * TOK + (r + 1) * WIN].astype(BF)
-            out_ref[r, pl.ds(w * WIN, WIN), C:] = ocean[r * WIN : (r + 1) * WIN, w * 128 : (w + 1) * 128].astype(BF)
+    step = pl.program_id(0)
+    last = pl.num_programs(0) - 1
+
+    def enter():
+        flags = (1 - land_ref[...]).astype(F32)
+        rows = jnp.broadcast_to(flags[:, None, :], (WIN, WIN, windows * WIN)).reshape(TOK, windows * WIN)
+        ocean_ref[...] = dot_nn((rows * spread_ref[...]).astype(BF), pick_ref[...])
+        for r in range(WIN):
+            for w in range(windows):
+                xw_ref[pl.ds(w * TOK + r * WIN, WIN), :] = x_ref[0, r, pl.ds(w * WIN, WIN), :].astype(F32)
+
+    def pack():
+        project(xw_ref[...], gain_ref[0:1], qkv_ref, wt_ref, qt_ref, k_ref, vt_ref)
+
+    def store(r, tile, value):
+        out_ref[r, pl.ds(tile * WIN, WIN), :C] = value
+        out_ref[r, pl.ds(tile * WIN, WIN), C:] = flag_ref[pl.ds(r * WIN, WIN), pl.ds(tile * 128, 128)].astype(BF)
+
+    def turn():
+        mixed_ref[...] = ot_ref[...].astype(BF).T
+
+    def leave():
+        flag_ref[...] = ocean_ref[...]
+
+    attend = attend_stages(qt_ref, k_ref, vt_ref, bias_ref, s_ref, p_ref, ot_ref, lambda w: ocean_ref[:, pl.ds(w * 128, 128)], windows // 2)
+    first = [enter, pack, *attend, turn]
+    second = finish_stages(lambda r, t: before_ref[0, r, pl.ds(t * WIN, WIN), :], mixed_ref, mid_ref, n_ref, hid_ref,
+                           proj_ref, gain_ref[1:2], up_ref, down_ref, store)
+
+    @pl.when(step == 0)
+    def _():
+        prepare(qkv_ref, table_ref, select_ref, wt_ref, tab_ref, row_ref, bias_ref)
+        run("", first, [])
+        leave()
+
+    @pl.when((step > 0) & (step < last))
+    def _():
+        run(ORDER_FIRST, first, second)
+        leave()
+
+    @pl.when(step == last)
+    def _():
+        run("", [], second)
 
 
 def second_kernel(low_ref, high_ref, low_side_ref, high_side_ref, above_ref, below_ref, own_ref,
                   gain_ref, qkv_ref, table_ref, select_ref, proj_ref, up_ref, down_ref,
-                  out_ref, wt_ref, tab_ref, row_ref, bias_ref, xw_ref, qt_ref, k_ref, vt_ref, s_ref, p_ref, ot_ref, o_ref, att_ref):
+                  out_ref, wt_ref, tab_ref, row_ref, bias_ref, xw_ref, qt_ref, k_ref, vt_ref, s_ref, p_ref, ot_ref,
+                  mixed_ref, mid_ref, n_ref, hid_ref, o_ref, carry_ref):
     windows = 9
     step = pl.program_id(0)
-    last = step == pl.num_programs(0) - 1
-    prepare(qkv_ref, table_ref, select_ref, wt_ref, tab_ref, row_ref, bias_ref)
-    low = lax.broadcasted_iota(jnp.int32, (WIN, C), 0) < SHIFT
+    last = pl.num_programs(0) - 1
     low_wide = lax.broadcasted_iota(jnp.int32, (WIN, WIDE), 0) < SHIFT
-    for r in range(WIN):
-        near, side, far, edge = (low_ref, low_side_ref, above_ref, step == 0) if r < SHIFT else (high_ref, high_side_ref, below_ref, last)
-        tiles = []
-        for t in range(windows):
-            inner = near[r % SHIFT, pl.ds(t * WIN, WIN), :] if t < 8 else side[r % SHIFT]
-            tiles.append(jnp.where(edge, far[r % SHIFT, pl.ds(t * WIN, WIN), :].astype(F32), inner.astype(F32)))
-        for w in range(windows):
-            xw_ref[pl.ds(w * TOK + r * WIN, WIN), :] = jnp.where(low_wide, tiles[w], tiles[(w - 1) % windows])
-    xw_ref[pl.ds(windows * TOK, TOK), :] = jnp.zeros((TOK, WIDE), F32)
-    project(xw_ref[:, :C], gain_ref[2:3], qkv_ref, wt_ref, qt_ref, k_ref, vt_ref)
-    attend(qt_ref, k_ref, vt_ref, bias_ref, s_ref, p_ref, ot_ref, lambda w: xw_ref[pl.ds(w * TOK, TOK), C:], 5)
-    o_ref[...] = ot_ref[...].T
-    for t in range(8):
+    low = lax.broadcasted_iota(jnp.int32, (TOK, C), 0) % WIN < SHIFT
+
+    def enter():
         for r in range(WIN):
-            left = o_ref[pl.ds(t * TOK + r * WIN, WIN), :]
-            right = o_ref[pl.ds((t + 1) * TOK + r * WIN, WIN), :]
-            att_ref[r + SHIFT, pl.ds(t * WIN, WIN), :] = jnp.where(low, left, right)
-
-    @pl.when(step > 0)
-    def _():
-        mixed = att_ref[0:WIN].reshape(WIN * 64, C).astype(BF)
-        x = own_ref[...].astype(F32).reshape(WIN * 64, C)
-        result = finish(x, mixed, proj_ref, gain_ref[3:4], up_ref, down_ref)
-        out_ref[0] = result.reshape(WIN, 64, C).astype(BF)
-
-    att_ref[0:SHIFT] = att_ref[WIN : WIN + SHIFT]
+            near, side, far, edge = (low_ref, low_side_ref, above_ref, step == 0) if r < SHIFT else (high_ref, high_side_ref, below_ref, step == last - 1)
+            tiles = []
+            for t in range(windows):
+                inner = near[r % SHIFT, pl.ds(t * WIN, WIN), :] if t < 8 else side[r % SHIFT]
+                tiles.append(jnp.where(edge, far[r % SHIFT, pl.ds(t * WIN, WIN), :].astype(F32), inner.astype(F32)))
+            for w in range(windows):
+                xw_ref[pl.ds(w * TOK + r * WIN, WIN), :] = jnp.where(low_wide, tiles[w], tiles[(w - 1) % windows])
+
+    def pack():
+        project(xw_ref[:, :C], gain_ref[2:3], qkv_ref, wt_ref, qt_ref, k_ref, vt_ref)
+
+    def store(r, tile, value):
+        out_ref[0, r, pl.ds(tile * WIN, WIN), :] = value
+
+    def turn():
+        o_ref[...] = ot_ref[...].T
+        for t in range(8):
+            rows = jnp.where(low, o_ref[pl.ds(t * TOK, TOK), :], o_ref[pl.ds((t + 1) * TOK, TOK), :]).astype(BF)
+            mixed_ref[pl.ds(t * TOK, TOK // 2), :] = carry_ref[pl.ds(t * TOK // 2, TOK // 2), :]
+            mixed_ref[pl.ds(t * TOK + TOK // 2, TOK // 2), :] = rows[: TOK // 2]
+            carry_ref[pl.ds(t * TOK // 2, TOK // 2), :] = rows[TOK // 2 :]
+
+    attend = attend_stages(qt_ref, k_ref, vt_ref, bias_ref, s_ref, p_ref, ot_ref, lambda w: xw_ref[pl.ds(w * TOK, TOK), C:], 5)
+    first = [enter, pack, *attend, turn]
+    second = finish_stages(lambda r, t: own_ref[r, pl.ds(t * WIN, WIN), :], mixed_ref, mid_ref, n_ref, hid_ref,
+                           proj_ref, gain_ref[3:4], up_ref, down_ref, store)
+
+    @pl.when(step == 0)
+    def _():
+        prepare(qkv_ref, table_ref, select_ref, wt_ref, tab_ref, row_ref, bias_ref)
+        xw_ref[pl.ds(windows * TOK, TOK), :] = jnp.zeros((TOK, WIDE), F32)
+        carry_ref[...] = jnp.zeros_like(carry_ref)
+
+    @pl.when(step < 2)
+    def _():
+        run("", first, [])
+
+    @pl.when((step >= 2) & (step < last))
+    def _():
+        run(ORDER_SECOND, first, second)
+
+    @pl.when(step == last)
+    def _():
+        run("", [], second)
 
 
 def whole(*shape):
@@ -242,6 +319,10 @@
         pltpu.VMEM((2, HEADS, TOK, 128), F32),
         pltpu.VMEM((2, HEADS // 2, 128, 256), BF),
         pltpu.VMEM((C, tokens), F32),
+        pltpu.VMEM((8 * TOK, C), BF),
+        pltpu.VMEM((8 * TOK, C), F32),
+        pltpu.VMEM((8 * TOK, C), BF),
+        pltpu.VMEM((8 * TOK, HID), BF),
     ]
 
 
@@ -252,35 +333,37 @@
     _, rows, cols, _ = fields.shape
     windows = cols // WIN
     tokens = windows * TOK
+    bands = rows // WIN
     spread, pick = flag_matrices(windows)
     return pl.pallas_call(
         first_kernel,
-        grid=(rows // WIN,),
+        grid=(bands + 1,),
         in_specs=[
-            pl.BlockSpec((1, WIN, cols, C), lambda i: (0, i, 0, 0)),
-            pl.BlockSpec((WIN, cols), lambda i: (i, 0)),
+            pl.BlockSpec((1, WIN, cols, C), lambda i: (0, jnp.minimum(i, bands - 1), 0, 0)),
+            pl.BlockSpec((1, WIN, cols, C), lambda i: (0, jnp.maximum(i - 1, 0), 0, 0)),
+            pl.BlockSpec((WIN, cols), lambda i: (jnp.minimum(i, bands - 1), 0)),
             *weight_specs(0),
             whole(*spread.shape),
             whole(*pick.shape),
         ],
-        out_specs=pl.BlockSpec((WIN, cols, WIDE), lambda i: (i, 0, 0)),
+        out_specs=pl.BlockSpec((WIN, cols, WIDE), lambda i: (jnp.maximum(i - 1, 0), 0, 0)),
         out_shape=jax.ShapeDtypeStruct((rows, cols, WIDE), BF),
-        scratch_shapes=[*scratch(tokens, C), pltpu.VMEM((tokens, C), BF)],
+        scratch_shapes=[*scratch(tokens, C), pltpu.VMEM((TOK, windows * 128), F32), pltpu.VMEM((TOK, windows * 128), F32)],
         compiler_params=PARAMS,
         name="first_layer",
-    )(fields, land, *weights(False), jnp.asarray(spread), jnp.asarray(pick, BF))
+    )(fields, fields, land, *weights(False), jnp.asarray(spread), jnp.asarray(pick, BF))
 
 
 def second_layer(own, side, above, below, weights):
     rows, cols, _ = own.shape
     bands = rows // WIN
     tokens = (cols // WIN + 2) * TOK
-    lower = lambda i: (jnp.maximum(2 * i - 1, 0), 0, 0)
+    lower = lambda i: (jnp.clip(2 * i - 1, 0, 2 * bands - 1), 0, 0)
     upper = lambda i: (jnp.minimum(2 * i, 2 * bands - 1), 0, 0)
-    done = lambda i: jnp.maximum(i - 1, 0)
+    done = lambda i: jnp.maximum(i - 2, 0)
     return pl.pallas_call(
         second_kernel,
-        grid=(bands + 1,),
+        grid=(bands + 2,),
         in_specs=[
             pl.BlockSpec((SHIFT, cols, WIDE), lower),
             pl.BlockSpec((SHIFT, cols, WIDE), upper),
@@ -293,7 +376,7 @@
         ],
         out_specs=pl.BlockSpec((1, WIN, cols, C), lambda i: (0, done(i), 0, 0)),
         out_shape=jax.ShapeDtypeStruct((1, rows, cols, C), BF),
-        scratch_shapes=[*scratch(tokens, WIDE), pltpu.VMEM((tokens, C), F32), pltpu.VMEM((WIN + SHIFT, cols, C), F32)],
+        scratch_shapes=[*scratch(tokens, WIDE), pltpu.VMEM((tokens, C), F32), pltpu.VMEM((bands * TOK // 2, C), BF)],
         compiler_params=PARAMS,
         name="second_layer",
     )(own, own, side, side, above, below, own, *weights(True))

time: 117 us -> 107 us (0.915)
  Pallas kernels: 90.8 us -> 81.5 us
    pallas_call x2, Pallas kernels: 90.8 us -> 81.5 us  [the longest x1 44.8 us: second_layer(): pl.pallas_call(second_kernel, grid=(bands + 2,), in_specs=[pl.BlockSpec((...]
where the time goes in v2:
time: 107 us
  Pallas kernels  81.5 us (76%)
  waiting for transfers between devices  11.7 us (11%)
  starting transfers between devices  8.24 us (8%)
  local copies, waits for them, and re-layouts  4.53 us (4%)
  other arithmetic  1.15 us (1%)
    pallas_call x1, Pallas kernels, second_layer(): pl.pallas_call(second_kernel, grid=(bands + 2,), in_specs=[pl.BlockSpec((...  44.8 us
    pallas_call x1, Pallas kernels, first_layer(): pl.pallas_call(first_kernel, grid=(bands + 1,), in_specs=[pl.BlockSpec((1...  36.7 us
    ppermute x1, waiting for transfers between devices, borders(): lax.ppermute(jnp.concatenate([block[:SHIFT], side[:SHIFT]], axis=1), 'lat...  4.26 us
    ppermute x1, starting transfers between devices, borders(): lax.ppermute(jnp.concatenate([block[:SHIFT], side[:SHIFT]], axis=1), 'lat...  3.91 us
    ppermute x1, waiting for transfers between devices, borders(): left = lax.ppermute(block[:, -SHIFT:], 'lon', forward)  3.12 us
    ppermute x1, waiting for transfers between devices, borders(): right = lax.ppermute(block[:, :SHIFT], 'lon', backward)  2.82 us
    ppermute x1, starting transfers between devices, borders(): right = lax.ppermute(block[:, :SHIFT], 'lon', backward)  2.21 us
  transfers between devices with their start and end apart: 4, of which 4 were waited for; matrix products, arithmetic and copies ran while one was open for 2% of the time, Pallas kernels for 0%

profile of v2, /device:TPU:104, one launch (start us, length us, event | category | flops | bytes accessed | tf_op | source)
XLA Modules:
  0.0 107.2 jit_solution(5547251685839401905)
XLA Ops:
  0.0 1.4 %copy.13.table_ref = f32[2,12,225]{2,1,0:T(8,128)} copy(f32[2,12,225]{2,0,1:T(2,128)} %param.16) | data formatting | bytes 43200 | tf_op args[4]
  1.4 36.7 %first_layer.1.low_ref.high_ref.own_ref = bf16[64,64,512]{2,1,0:T(8,128)(2,1)} custom-call(bf16[1,64,64,384]{3,2,1,0:T(8,128)(2,1)} %before_ref.1, bf16[1,64,64,384]{3,2,1,0:T(8,128)(2,1)} %before_ref.1, s32[64,64]{1,0:T(8,128)} %land_ref.1, f32[4,384]{1,0:T(4,128)} %gain_ref.3, bf16[2,384,1152]{2,1,0:T(8,128)(2,1)} %qkv_ref.3, ...), custom_call_target="tpu_custom_call" | custom-call | tf_op jit(solution)/shard_map/first_layer/pallas_call | solution.py:338
  38.1 1.4 %fusion.3 = (bf16[64,4,512]{2,1,0:T(4,128)(2,1)S(1)}, bf16[64,4,512]{2,1,0:T(4,128)(2,1)S(1)}) fusion(bf16[64,64,512]{2,1,0:T(8,128)(2,1)} %first_layer.1.low_ref.high_ref.own_ref), kind=kLoop, calls=%fused_computation.10 | loop fusion | bytes 1048576 | tf_op jit(solution)/shard_map/slice | solution.py:396
  39.5 2.2 %collective-permute-start = (bf16[64,4,512]{2,1,0:T(4,128)(2,1)S(1)}, bf16[64,4,512]{2,1,0:T(4,128)(2,1)S(1)}, u32[]{:S(2)}, u32[]{:S(2)}) collective-permute-start(bf16[64,4,512]{2,1,0:T(4,128)(2,1)S(1)} %get-tuple-element.7), channel_id=1, source_target_pairs={{1,0},{2,1},{3,2},{4,3},{5,4},{6,5},{7,6},{0,7},{9,8},{10,9},{11,1... | collective-permute-start | bytes 786440 | tf_op jit(solution)/shard_map/ppermute | solution.py:396
  41.7 0.0 collective-permute-start.1
  41.7 1.1 fusion.2
  42.8 2.8 %collective-permute-done = bf16[64,4,512]{2,1,0:T(4,128)(2,1)S(1)} collective-permute-done((bf16[64,4,512]{2,1,0:T(4,128)(2,1)S(1)}, bf16[64,4,512]{2,1,0:T(4,128)(2,1)S(1)}, u32[]{:S(2)}, u32[]{:S(2)}) %collective-permute-start) | collective-permute-done | bytes 262176 | tf_op jit(solution)/shard_map/ppermute | solution.py:396
  45.6 3.1 %collective-permute-done.1 = bf16[64,4,512]{2,1,0:T(4,128)(2,1)S(1)} collective-permute-done((bf16[64,4,512]{2,1,0:T(4,128)(2,1)S(1)}, bf16[64,4,512]{2,1,0:T(4,128)(2,1)S(1)}, u32[]{:S(2)}, u32[]{:S(2)}) %collective-permute-start.1) | collective-permute-done | bytes 262176 | tf_op jit(solution)/shard_map/ppermute | solution.py:395
  48.8 2.1 %collective-permute-start.2 = (bf16[4,72,512]{2,1,0:T(8,128)(2,1)S(1)}, bf16[4,72,512]{2,1,0:T(8,128)(2,1)S(1)}, u32[]{:S(2)}, u32[]{:S(2)}) collective-permute-start(bf16[4,72,512]{2,1,0:T(8,128)(2,1)S(1)} %pad_maximum_fusion.1), channel_id=1, source_target_pairs={{0,8},{8,16},{16,24},{24,32},{32,40},{40,48},{48,56},{56,64},{64,7... | collective-permute-start | bytes 884744 | tf_op jit(solution)/shard_map/ppermute | solution.py:399
  51.0 3.9 %collective-permute-start.3 = (bf16[4,72,512]{2,1,0:T(8,128)(2,1)S(1)}, bf16[4,72,512]{2,1,0:T(8,128)(2,1)S(1)}, u32[]{:S(2)}, u32[]{:S(2)}) collective-permute-start(bf16[4,72,512]{2,1,0:T(8,128)(2,1)S(1)} %pad_maximum_fusion.2), channel_id=1, source_target_pairs={{8,0},{16,8},{24,16},{32,24},{40,32},{48,40},{56,48},{64,56},{72,6... | collective-permute-start | bytes 884744 | tf_op jit(solution)/shard_map/ppermute | solution.py:400
  54.9 1.1 %pad_maximum_fusion.low_side_ref.high_side_ref = bf16[64,8,512]{2,1,0:T(8,128)(2,1)} fusion(bf16[64,4,512]{2,1,0:T(4,128)(2,1)S(1)} %collective-permute-done.1, bf16[64,4,512]{2,1,0:T(4,128)(2,1)S(1)} %collective-permute-done), kind=kLoop, calls=%fused_computation.2 | loop fusion | flops 1048576 | bytes 1048576 | tf_op jit(solution)/shard_map/concatenate | solution.py:397
  55.9 1.5 %collective-permute-done.2.above_ref = bf16[4,72,512]{2,1,0:T(8,128)(2,1)S(1)} collective-permute-done((bf16[4,72,512]{2,1,0:T(8,128)(2,1)S(1)}, bf16[4,72,512]{2,1,0:T(8,128)(2,1)S(1)}, u32[]{:S(2)}, u32[]{:S(2)}) %collective-permute-start.2) | collective-permute-done | bytes 294944 | tf_op jit(solution)/shard_map/ppermute | solution.py:399
  57.4 0.0 copy-start
  57.4 4.3 %collective-permute-done.3.below_ref = bf16[4,72,512]{2,1,0:T(8,128)(2,1)S(1)} collective-permute-done((bf16[4,72,512]{2,1,0:T(8,128)(2,1)S(1)}, bf16[4,72,512]{2,1,0:T(8,128)(2,1)S(1)}, u32[]{:S(2)}, u32[]{:S(2)}) %collective-permute-start.3) | collective-permute-done | bytes 294944 | tf_op jit(solution)/shard_map/ppermute | solution.py:400
  61.7 0.0 copy-done
  61.7 0.0 copy-start.1
  61.7 0.7 copy-done.1
  62.4 44.8 %second_layer.1 = bf16[1,64,64,384]{3,2,1,0:T(8,128)(2,1)} custom-call(bf16[64,64,512]{2,1,0:T(8,128)(2,1)} %first_layer.1.low_ref.high_ref.own_ref, bf16[64,64,512]{2,1,0:T(8,128)(2,1)} %first_layer.1.low_ref.high_ref.own_ref, bf16[64,8,512]{2,1,0:T(8,128)(2,1)} %pad_maximum_fusion.low_side_ref.high_side_ref, ...), custom_call_target="tpu_custom_call" | custom-call | tf_op jit(solution)/shard_map/second_layer/pallas_call | solution.py:364
  (3 shorter events, 0.1 us)
Async XLA Ops:
  39.5 6.1 %collective-permute-start = (bf16[64,4,512]{2,1,0:T(4,128)(2,1)S(1)}, bf16[64,4,512]{2,1,0:T(4,128)(2,1)S(1)}, u32[]{:S(2)}, u32[]{:S(2)}) collective-permute-start(bf16[64,4,512]{2,1,0:T(4,128)(2,1)S(1)} %get-tuple-element.7), channel_id=1, source_target_pairs={{1,0},{2,1},{3,2},{4,3},{5,4},{6,5},{7,6},{0,7},{9,8},{10,9},{11,1... | collective-permute-start | bytes 786440 | tf_op jit(solution)/shard_map/ppermute | solution.py:396
  41.7 7.0 %collective-permute-start.1 = (bf16[64,4,512]{2,1,0:T(4,128)(2,1)S(1)}, bf16[64,4,512]{2,1,0:T(4,128)(2,1)S(1)}, u32[]{:S(2)}, u32[]{:S(2)}) collective-permute-start(bf16[64,4,512]{2,1,0:T(4,128)(2,1)S(1)} %get-tuple-element.8), channel_id=1, source_target_pairs={{0,1},{1,2},{2,3},{3,4},{4,5},{5,6},{6,7},{7,0},{8,9},{9,10},{10,1... | collective-permute-start | bytes 786440 | tf_op jit(solution)/shard_map/ppermute | solution.py:395
  48.8 8.6 %collective-permute-start.2 = (bf16[4,72,512]{2,1,0:T(8,128)(2,1)S(1)}, bf16[4,72,512]{2,1,0:T(8,128)(2,1)S(1)}, u32[]{:S(2)}, u32[]{:S(2)}) collective-permute-start(bf16[4,72,512]{2,1,0:T(8,128)(2,1)S(1)} %pad_maximum_fusion.1), channel_id=1, source_target_pairs={{0,8},{8,16},{16,24},{24,32},{32,40},{40,48},{48,56},{56,64},{64,7... | collective-permute-start | bytes 884744 | tf_op jit(solution)/shard_map/ppermute | solution.py:399
  51.0 10.7 %collective-permute-start.3 = (bf16[4,72,512]{2,1,0:T(8,128)(2,1)S(1)}, bf16[4,72,512]{2,1,0:T(8,128)(2,1)S(1)}, u32[]{:S(2)}, u32[]{:S(2)}) collective-permute-start(bf16[4,72,512]{2,1,0:T(8,128)(2,1)S(1)} %pad_maximum_fusion.2), channel_id=1, source_target_pairs={{8,0},{16,8},{24,16},{32,24},{40,32},{48,40},{56,48},{64,56},{72,6... | collective-permute-start | bytes 884744 | tf_op jit(solution)/shard_map/ppermute | solution.py:400
  57.4 4.3 %copy-start = (bf16[4,72,512]{2,1,0:T(8,128)(2,1)}, bf16[4,72,512]{2,1,0:T(8,128)(2,1)S(1)}, u32[]{:S(2)}) copy-start(bf16[4,72,512]{2,1,0:T(8,128)(2,1)S(1)} %collective-permute-done.2.above_ref) | copy-start | bytes 884740
  61.7 0.7 copy-start.1

commit v3 on v2

v3 whole, which is shorter than its diff:
```python
import functools

import jax
import jax.numpy as jnp
import numpy as np
from jax import lax
from jax.experimental import pallas as pl
from jax.experimental.pallas import tpu as pltpu
from jax.sharding import PartitionSpec as P

HEADS = 12
WIN = 8
SHIFT = 4
EPS = 1e-05
C = 384
HID = 1536
TOK = WIN * WIN
BIG = 1e30
LOG2E = 1.4426950408889634
QSCALE = LOG2E / (C // HEADS) ** 0.5
BF = jnp.bfloat16
UP_CHUNK = 256
FINE = True
LAG = 2
DOWN_PARTS = 2
AHEAD = 0.0
COSTS = (22, 22, 18)
F32 = jnp.float32


WIDE = C + 128
SPAN = 2 * WIN - 1


def bias_selector(shifted):
    slot = np.arange(WIN)
    col = (slot + SHIFT) % WIN if shifted else slot
    table = np.zeros((256, WIN, 128), np.float32)
    for key in range(WIN):
        for far in range(SPAN):
            for query in range(WIN):
                table[far * SPAN + col[query] - col[key] + WIN - 1, key, far * WIN + query] = 1.0
    return table.reshape(256, WIN * 128)


def flag_matrices(windows):
    slot = np.arange(TOK) % WIN
    lane = np.arange(windows * WIN)
    spread = lane[None, :] % WIN == slot[:, None]
    pick = lane[:, None] // WIN == np.repeat(np.arange(windows), 128)[None, :]
    return spread.astype(np.float32), pick.astype(np.float32)


def normed(values, gain):
    center = jnp.mean(values, axis=-1, keepdims=True)
    moved = values - center
    spread = jnp.mean(moved * moved, axis=-1, keepdims=True)
    return (moved * lax.rsqrt(spread + EPS) * gain).astype(BF)


def dot_nt(a, b):
    return lax.dot_general(a, b, (((1,), (1,)), ((), ())), preferred_element_type=F32)


def dot_nn(a, b):
    return jnp.dot(a, b, preferred_element_type=F32)


def score_two(qt_ref, k_ref, bias_ref, s_ref, mask_ref, pair, two):
    here = pl.ds(pair * 128, 128)
    first = lax.broadcasted_iota(jnp.int32, (TOK, 128), 1) < TOK
    zero = jnp.zeros((32, 128), BF)
    keys = k_ref[here, pl.ds(two // 2 * 128, 128)]
    columns = []
    for j in range(2):
        blocks = [zero] * 4
        blocks[two % 2 * 2 + j] = qt_ref[pl.ds((2 * two + j) * 32, 32), here]
        columns.append(jnp.concatenate(blocks, axis=0))
    scores = dot_nn(keys, jnp.concatenate(columns, axis=1))
    for j in range(2):
        both = scores[:, j * 128 : (j + 1) * 128]
        s_ref[pair % 2, 2 * two + j] = jnp.where(first, both[:TOK], both[TOK:]) + (bias_ref[2 * two + j] + mask_ref[pair % 2])


def weigh_head(s_ref, p_ref, pair, head):
    side = lax.broadcasted_iota(jnp.int32, (1, 128), 1) < TOK
    s = s_ref[pair % 2, head]
    e = jnp.exp2(s - jnp.max(s, axis=0, keepdims=True))
    inv = 1.0 / jnp.sum(e, axis=0, keepdims=True)
    lanes = pl.ds(head % 2 * 128, 128)
    p_ref[pair % 2, head // 2, :TOK, lanes] = (e * jnp.where(side, inv, 0.0)).astype(BF)
    p_ref[pair % 2, head // 2, TOK:, lanes] = (e * jnp.where(side, 0.0, inv)).astype(BF)


def mix_two(vt_ref, p_ref, ot_ref, pair, two):
    here = pl.ds(pair * 128, 128)
    mixed = dot_nn(vt_ref[pl.ds(two * 64, 64), here], p_ref[pair % 2, two])
    ot_ref[pl.ds(two * 64, 32), here] = mixed[:32, :128]
    ot_ref[pl.ds(two * 64 + 32, 32), here] = mixed[32:, 128:]


def attend_stages(qt_ref, k_ref, vt_ref, bias_ref, s_ref, p_ref, ot_ref, mask_ref, ocean, pairs):
    key = lax.broadcasted_iota(jnp.int32, (TOK, 128), 0)
    lane = lax.broadcasted_iota(jnp.int32, (TOK, 128), 1)
    half = HEADS // 2

    def mask(pair):
        flags = jnp.where(lane < TOK, ocean(2 * pair), ocean(2 * pair + 1))
        mask_ref[pair % 2] = jnp.where((lane % TOK == key) | (flags > 0.5), 0.0, -BIG)

    def score(pair, two):
        if two == 0:
            mask(pair)
        score_two(qt_ref, k_ref, bias_ref, s_ref, mask_ref, pair, two)

    def weigh(pair, two):
        weigh_head(s_ref, p_ref, pair, 2 * two)
        weigh_head(s_ref, p_ref, pair, 2 * two + 1)

    stages = [(COSTS[0], functools.partial(score, 0, two)) for two in range(half)]
    for pair in range(pairs):
        if FINE:
            for two in range(half):
                if pair + 1 < pairs:
                    stages.append((COSTS[0], functools.partial(score, pair + 1, two)))
                stages.append((COSTS[1], functools.partial(weigh, pair, two)))
                if two >= LAG:
                    stages.append((COSTS[2], functools.partial(mix_two, vt_ref, p_ref, ot_ref, pair, two - LAG)))
            for two in range(half - LAG, half):
                stages.append((COSTS[2], functools.partial(mix_two, vt_ref, p_ref, ot_ref, pair, two)))
        else:
            if pair + 1 < pairs:
                stages += [(COSTS[0], functools.partial(score, pair + 1, two)) for two in range(half)]
            stages += [(COSTS[1], functools.partial(weigh, pair, two)) for two in range(half)]
            stages += [(COSTS[2], functools.partial(mix_two, vt_ref, p_ref, ot_ref, pair, two)) for two in range(half)]
    return stages


def finish_stages(x_tile, mixed_ref, mid_ref, n_ref, hid_ref, proj_ref, gain, up_ref, down_ref, store):
    def head():
        for tile in range(8):
            for r in range(WIN):
                mid_ref[pl.ds(tile * TOK + r * WIN, WIN), :] = x_tile(r, tile).astype(F32)
        mid_ref[...] = (mid_ref[...] + dot_nn(mixed_ref[...], proj_ref[...])).astype(BF).astype(F32)

    def norm(at):
        rows = pl.ds(at, 128)
        n_ref[rows, :] = normed(mid_ref[rows, :], gain)

    def up(at):
        lanes = pl.ds(at, UP_CHUNK)
        hid_ref[:, lanes] = jax.nn.gelu(dot_nn(n_ref[...], up_ref[:, lanes]), approximate=True).astype(BF)

    def down(part):
        rows = 8 * TOK // DOWN_PARTS
        here = pl.ds(part * rows, rows)
        result = mid_ref[here, :] + dot_nn(hid_ref[here, :], down_ref[...])
        for tile in range(8 // DOWN_PARTS):
            for r in range(WIN):
                store(r, part * 8 // DOWN_PARTS + tile, result[tile * TOK + r * WIN : tile * TOK + (r + 1) * WIN])

    return (
        [(300, head)]
        + [(40, functools.partial(norm, at)) for at in range(0, 8 * TOK, 128)]
        + [(0.7 * UP_CHUNK, functools.partial(up, at)) for at in range(0, HID, UP_CHUNK)]
        + [(800 // DOWN_PARTS, functools.partial(down, part)) for part in range(DOWN_PARTS)]
    )


def run(first, second, shift=0.0):
    ends = []
    for which, stages, ahead in ((0, first, 0.0), (1, second, shift)):
        total = sum(cost for cost, _ in stages) or 1
        done = 0
        for cost, stage in stages:
            done += cost
            ends.append(((done - cost * 0.5) / total - ahead, which, len(ends), stage))
    for _, _, _, stage in sorted(ends, key=lambda e: e[:3]):
        stage()


def project_stages(x_ref, packed_ref, gain, qkv_ref, wt_ref, qt_ref, k_ref, vt_ref):
    def norm(at):
        rows = pl.ds(at, 128)
        packed_ref[rows, :] = normed(x_ref[rows, :C], gain)

    def queries():
        qt_ref[...] = (dot_nt(wt_ref[:C], packed_ref[...]) * QSCALE).astype(BF)

    def keys():
        k_ref[...] = dot_nn(packed_ref[...], qkv_ref[:, C : 2 * C]).astype(BF)

    def values():
        vt_ref[...] = dot_nt(wt_ref[C:], packed_ref[...]).astype(BF)

    tokens = packed_ref.shape[0]
    return [(40, functools.partial(norm, at)) for at in range(0, tokens, 128)] + [(250, keys), (250, queries), (250, values)]


def prepare(layer, qkv_ref, table_ref, select_ref, wt_ref, tab_ref, row_ref, bias_ref):
    wt_ref[:C] = qkv_ref[:, :C].T
    wt_ref[C:] = qkv_ref[:, 2 * C :].T
    tab_ref[...] = jnp.zeros_like(tab_ref)
    tab_ref[:HEADS, : SPAN * SPAN] = table_ref[:, layer] * LOG2E
    high = tab_ref[...].astype(BF)
    low = (tab_ref[...] - high.astype(F32)).astype(BF)
    picked = dot_nn(high, select_ref[...]) + dot_nn(low, select_ref[...])
    for key in range(WIN):
        for head in range(HEADS):
            row_ref[head, key : key + 1] = picked[head : head + 1, key * 128 : (key + 1) * 128]
    first = lax.broadcasted_iota(jnp.int32, (WIN, 128), 1) < TOK
    for head in range(HEADS):
        rows = row_ref[head]
        for row in range(WIN):
            back = (WIN - 1 - row) * WIN
            left = pltpu.roll(rows, (128 - back) % 128, 1)
            right = pltpu.roll(rows, (TOK - back) % 128, 1)
            bias_ref[head, row * WIN : (row + 1) * WIN] = jnp.where(first, left, right)


def first_kernel(x_ref, before_ref, land_ref, gain_ref, qkv_ref, table_ref, select_ref, proj_ref, up_ref, down_ref, spread_ref, pick_ref,
                 out_ref, begin_ref, end_ref, wt_ref, tab_ref, row_ref, bias_ref, xw_ref, qt_ref, k_ref, vt_ref, s_ref, p_ref, ot_ref,
                 packed_ref, mask_ref, mixed_ref, mid_ref, n_ref, hid_ref, ocean_ref, flag_ref):
    windows = 8
    step = pl.program_id(0)
    last = pl.num_programs(0) - 1

    def enter():
        flags = (1 - land_ref[...]).astype(F32)
        rows = jnp.broadcast_to(flags[:, None, :], (WIN, WIN, windows * WIN)).reshape(TOK, windows * WIN)
        ocean_ref[...] = dot_nn((rows * spread_ref[...]).astype(BF), pick_ref[...])
        for r in range(WIN):
            for w in range(windows):
                xw_ref[pl.ds(w * TOK + r * WIN, WIN), :] = x_ref[0, r, pl.ds(w * WIN, WIN), :].astype(F32)

    def store(r, tile, value):
        flag = flag_ref[pl.ds(r * WIN, WIN), pl.ds(tile * 128, 128)]
        out_ref[r, pl.ds(tile * WIN, WIN), :C] = value.astype(BF)
        out_ref[r, pl.ds(tile * WIN, WIN), C:] = flag.astype(BF)
        if tile == 0:
            begin_ref[r, :, :C] = value[:SHIFT].astype(BF)
            begin_ref[r, :, C:] = flag[:SHIFT].astype(BF)
        if tile == windows - 1:
            end_ref[r, :, :C] = value[SHIFT:].astype(BF)
            end_ref[r, :, C:] = flag[SHIFT:].astype(BF)

    def turn():
        mixed_ref[...] = ot_ref[...].astype(BF).T

    def leave():
        flag_ref[...] = ocean_ref[...]

    attend = attend_stages(qt_ref, k_ref, vt_ref, bias_ref, s_ref, p_ref, ot_ref, mask_ref, lambda w: ocean_ref[:, pl.ds(w * 128, 128)], windows // 2)
    pack = project_stages(xw_ref, packed_ref, gain_ref[0:1], qkv_ref, wt_ref, qt_ref, k_ref, vt_ref)
    first = [(200, enter), *pack, *attend, (150, turn)]
    second = finish_stages(lambda r, t: before_ref[0, r, pl.ds(t * WIN, WIN), :], mixed_ref, mid_ref, n_ref, hid_ref,
                           proj_ref, gain_ref[1:2], up_ref, down_ref, store)

    @pl.when(step == 0)
    def _():
        prepare(0, qkv_ref, table_ref, select_ref, wt_ref, tab_ref, row_ref, bias_ref)
        run(first, [])
        leave()

    @pl.when((step > 0) & (step < last))
    def _():
        run(first, second, AHEAD)
        leave()

    @pl.when(step == last)
    def _():
        run([], second)


def second_kernel(low_ref, high_ref, low_right_ref, high_right_ref, low_left_ref, high_left_ref, above_ref, below_ref, own_ref,
                  gain_ref, qkv_ref, table_ref, select_ref, proj_ref, up_ref, down_ref,
                  out_ref, wt_ref, tab_ref, row_ref, bias_ref, xw_ref, qt_ref, k_ref, vt_ref, s_ref, p_ref, ot_ref, packed_ref, mask_ref,
                  mixed_ref, mid_ref, n_ref, hid_ref, o_ref, carry_ref):
    windows = 9
    step = pl.program_id(0)
    last = pl.num_programs(0) - 1
    low_wide = lax.broadcasted_iota(jnp.int32, (WIN, WIDE), 0) < SHIFT
    low = lax.broadcasted_iota(jnp.int32, (TOK, C), 0) % WIN < SHIFT

    def enter():
        for r in range(WIN):
            near, right, left, far, edge = (
                (low_ref, low_right_ref, low_left_ref, above_ref, step == 0)
                if r < SHIFT
                else (high_ref, high_right_ref, high_left_ref, below_ref, step == last - 1)
            )
            tiles = []
            for t in range(windows):
                if t < 8:
                    inner = near[r % SHIFT, pl.ds(t * WIN, WIN), :].astype(F32)
                else:
                    inner = jnp.concatenate([right[r % SHIFT].astype(F32), left[r % SHIFT].astype(F32)], axis=0)
                tiles.append(jnp.where(edge, far[r % SHIFT, pl.ds(t * WIN, WIN), :].astype(F32), inner))
            for w in range(windows):
                xw_ref[pl.ds(w * TOK + r * WIN, WIN), :] = jnp.where(low_wide, tiles[w], tiles[(w - 1) % windows])

    def store(r, tile, value):
        out_ref[0, r, pl.ds(tile * WIN, WIN), :] = value.astype(BF)

    def turn():
        o_ref[...] = ot_ref[...].T
        for t in range(8):
            rows = jnp.where(low, o_ref[pl.ds(t * TOK, TOK), :], o_ref[pl.ds((t + 1) * TOK, TOK), :]).astype(BF)
            mixed_ref[pl.ds(t * TOK, TOK // 2), :] = carry_ref[pl.ds(t * TOK // 2, TOK // 2), :]
            mixed_ref[pl.ds(t * TOK + TOK // 2, TOK // 2), :] = rows[: TOK // 2]
            carry_ref[pl.ds(t * TOK // 2, TOK // 2), :] = rows[TOK // 2 :]

    attend = attend_stages(qt_ref, k_ref, vt_ref, bias_ref, s_ref, p_ref, ot_ref, mask_ref, lambda w: xw_ref[pl.ds(w * TOK, TOK), C:], 5)
    pack = project_stages(xw_ref, packed_ref, gain_ref[2:3], qkv_ref, wt_ref, qt_ref, k_ref, vt_ref)
    first = [(250, enter), *pack, *attend, (200, turn)]
    second = finish_stages(lambda r, t: own_ref[r, pl.ds(t * WIN, WIN), :], mixed_ref, mid_ref, n_ref, hid_ref,
                           proj_ref, gain_ref[3:4], up_ref, down_ref, store)

    @pl.when(step == 0)
    def _():
        prepare(1, qkv_ref, table_ref, select_ref, wt_ref, tab_ref, row_ref, bias_ref)
        xw_ref[pl.ds(windows * TOK, TOK), :] = jnp.zeros((TOK, WIDE), F32)
        carry_ref[...] = jnp.zeros_like(carry_ref)

    @pl.when(step < 2)
    def _():
        run(first, [])

    @pl.when((step >= 2) & (step < last))
    def _():
        run(first, second, AHEAD)

    @pl.when(step == last)
    def _():
        run([], second)


def whole(*shape):
    return pl.BlockSpec(shape, lambda i: (0,) * len(shape), pipeline_mode=pl.Buffered(1))


def of_layer(layer, *shape):
    return pl.BlockSpec((None, *shape), lambda i: (layer, 0, 0), pipeline_mode=pl.Buffered(1))


def weight_specs(layer):
    return [
        whole(4, C),
        of_layer(layer, C, 3 * C),
        whole(HEADS, 2, SPAN * SPAN),
        whole(256, WIN * 128),
        of_layer(layer, C, C),
        of_layer(layer, C, HID),
        of_layer(layer, HID, C),
    ]


def scratch(tokens, width):
    return [
        pltpu.VMEM((2 * C, C), BF),
        pltpu.VMEM((16, 256), F32),
        pltpu.VMEM((HEADS, WIN, 128), F32),
        pltpu.VMEM((HEADS, TOK, 128), F32),
        pltpu.VMEM((tokens, width), F32),
        pltpu.VMEM((C, tokens), BF),
        pltpu.VMEM((tokens, C), BF),
        pltpu.VMEM((C, tokens), BF),
        pltpu.VMEM((2, HEADS, TOK, 128), F32),
        pltpu.VMEM((2, HEADS // 2, 128, 256), BF),
        pltpu.VMEM((C, tokens), F32),
        pltpu.VMEM((tokens, C), BF),
        pltpu.VMEM((2, TOK, 128), F32),
        pltpu.VMEM((8 * TOK, C), BF),
        pltpu.VMEM((8 * TOK, C), F32),
        pltpu.VMEM((8 * TOK, C), BF),
        pltpu.VMEM((8 * TOK, HID), BF),
    ]


PARAMS = pltpu.CompilerParams(vmem_limit_bytes=56 << 20)


def first_layer(fields, land, weights):
    _, rows, cols, _ = fields.shape
    windows = cols // WIN
    tokens = windows * TOK
    bands = rows // WIN
    spread, pick = flag_matrices(windows)
    return pl.pallas_call(
        first_kernel,
        grid=(bands + 1,),
        in_specs=[
            pl.BlockSpec((1, WIN, cols, C), lambda i: (0, jnp.minimum(i, bands - 1), 0, 0)),
            pl.BlockSpec((1, WIN, cols, C), lambda i: (0, jnp.maximum(i - 1, 0), 0, 0)),
            pl.BlockSpec((WIN, cols), lambda i: (jnp.minimum(i, bands - 1), 0)),
            *weight_specs(0),
            whole(*spread.shape),
            whole(*pick.shape),
        ],
        out_specs=[pl.BlockSpec((WIN, width, WIDE), lambda i: (jnp.maximum(i - 1, 0), 0, 0)) for width in (cols, SHIFT, SHIFT)],
        out_shape=[jax.ShapeDtypeStruct((rows, width, WIDE), BF) for width in (cols, SHIFT, SHIFT)],
        scratch_shapes=[*scratch(tokens, C), pltpu.VMEM((TOK, windows * 128), F32), pltpu.VMEM((TOK, windows * 128), F32)],
        compiler_params=PARAMS,
        name="first_layer",
    )(fields, fields, land, *weights(False), jnp.asarray(spread), jnp.asarray(pick, BF))


def second_layer(own, right, left, above, below, weights):
    rows, cols, _ = own.shape
    bands = rows // WIN
    tokens = (cols // WIN + 2) * TOK
    lower = lambda i: (jnp.clip(2 * i - 1, 0, 2 * bands - 1), 0, 0)
    upper = lambda i: (jnp.minimum(2 * i, 2 * bands - 1), 0, 0)
    done = lambda i: jnp.maximum(i - 2, 0)
    return pl.pallas_call(
        second_kernel,
        grid=(bands + 2,),
        in_specs=[
            pl.BlockSpec((SHIFT, cols, WIDE), lower),
            pl.BlockSpec((SHIFT, cols, WIDE), upper),
            pl.BlockSpec((SHIFT, SHIFT, WIDE), lower),
            pl.BlockSpec((SHIFT, SHIFT, WIDE), upper),
            pl.BlockSpec((SHIFT, SHIFT, WIDE), lower),
            pl.BlockSpec((SHIFT, SHIFT, WIDE), upper),
            pl.BlockSpec(memory_space=pltpu.VMEM),
            pl.BlockSpec(memory_space=pltpu.VMEM),
            pl.BlockSpec((WIN, cols, C), lambda i: (done(i), 0, 0)),
            *weight_specs(1),
        ],
        out_specs=pl.BlockSpec((1, WIN, cols, C), lambda i: (0, done(i), 0, 0)),
        out_shape=jax.ShapeDtypeStruct((1, rows, cols, C), BF),
        scratch_shapes=[*scratch(tokens, WIDE), pltpu.VMEM((tokens, C), F32), pltpu.VMEM((bands * TOK // 2, C), BF)],
        compiler_params=PARAMS,
        name="second_layer",
    )(own, own, right, right, left, left, above, below, own, *weights(True))


def ring(axis, periodic):
    count = lax.axis_size(axis)
    forward = [(i, i + 1) for i in range(count - 1)]
    if periodic:
        forward.append((count - 1, 0))
    return forward, [(b, a) for a, b in forward]


def borders(block, begin, end):
    forward, backward = ring("lon", True)
    left = lax.ppermute(end, "lon", forward)
    right = lax.ppermute(begin, "lon", backward)
    forward, backward = ring("lat", False)
    above = lax.ppermute(jnp.concatenate([part[-SHIFT:] for part in (block, right, left)], axis=1), "lat", forward)
    below = lax.ppermute(jnp.concatenate([part[:SHIFT] for part in (block, right, left)], axis=1), "lat", backward)
    return right, left, above, below


def shards(fields, land, norm_gains, qkv_weight, rel_bias, proj_weight, up_weight, down_weight):
    def weights(shifted):
        return (norm_gains, qkv_weight, rel_bias.transpose(1, 0, 2), jnp.asarray(bias_selector(shifted), BF), proj_weight, up_weight, down_weight)

    settled, begin, end = first_layer(fields, land, weights)
    return second_layer(settled, *borders(settled, begin, end), weights)


def solution(mesh):
    return jax.shard_map(
        shards,
        mesh=mesh,
        in_specs=(P(None, "lat", "lon", None), P("lat", "lon"), P(), P(), P(), P(), P(), P()),
        out_specs=P(None, "lat", "lon", None),
        check_vma=False,
    )
```

time: 107 us -> 105 us (0.981)
  local copies, waits for them, and re-layouts: 4.53 us -> 1.81 us
  waiting for transfers between devices: 11.7 us -> 12.9 us
  other arithmetic: 1.15 us -> 0.06 us
    slice x2 -> x3, local copies, waits for them, and re-layouts: 2.47 us -> 1.09 us  [borders(): part[:SHIFT]]
    unnamed x5 -> x8, local copies, waits for them, and re-layouts: 2.06 us -> 0.72 us
    ppermute x4, waiting for transfers between devices: 11.7 us -> 12.9 us  [the longest x1 4.28 us: borders(): lax.ppermute(jnp.concatenate([part[:SHIFT] for part in (block, right, lef...]
    concatenate x4 -> x2, other arithmetic: 1.15 us -> 0.06 us  [the longest x1 0.03 us: borders(): jnp.concatenate([part[-SHIFT:] for part in (block, right, left)], axis=1)]
  transfers between devices with their start and end apart: 4 -> 4, of which waited for: 4 -> 4; matrix products, arithmetic and copies ran while one was open for 2% -> 1% of each run, Pallas kernels for 0% -> 0%
where the time goes in v3:
time: 105 us
  Pallas kernels  81.5 us (78%)
  waiting for transfers between devices  12.9 us (12%)
  starting transfers between devices  8.24 us (8%)
  local copies, waits for them, and re-layouts  1.81 us (2%)
    pallas_call x1, Pallas kernels, second_layer(): pl.pallas_call(second_kernel, grid=(bands + 2,), in_specs=[pl.BlockSpec((...  45.2 us
    pallas_call x1, Pallas kernels, first_layer(): pl.pallas_call(first_kernel, grid=(bands + 1,), in_specs=[pl.BlockSpec((1...  36.4 us
    ppermute x1, waiting for transfers between devices, borders(): lax.ppermute(jnp.concatenate([part[:SHIFT] for part in (block, right, lef...  4.28 us
    ppermute x1, starting transfers between devices, borders(): lax.ppermute(jnp.concatenate([part[:SHIFT] for part in (block, right, lef...  3.9 us
    ppermute x1, waiting for transfers between devices, borders(): right = lax.ppermute(begin, 'lon', backward)  3.14 us
    ppermute x1, waiting for transfers between devices, borders(): left = lax.ppermute(end, 'lon', forward)  2.99 us
    ppermute x1, waiting for transfers between devices, borders(): lax.ppermute(jnp.concatenate([part[-SHIFT:] for part in (block, right, le...  2.54 us
    ppermute x1, starting transfers between devices, borders(): right = lax.ppermute(begin, 'lon', backward)  2.21 us
  transfers between devices with their start and end apart: 4, of which 4 were waited for; matrix products, arithmetic and copies ran while one was open for 1% of the time, Pallas kernels for 0%

profile of v3, /device:TPU:104, one launch (start us, length us, event | category | flops | bytes accessed | tf_op | source)
XLA Modules:
  0.0 104.6 jit_solution(10834826006724097304)
XLA Ops:
  0.0 36.4 %first_layer.1 = (bf16[64,64,512]{2,1,0:T(8,128)(2,1)}, bf16[64,4,512]{2,1,0:T(4,128)(2,1)}, bf16[64,4,512]{2,1,0:T(4,128)(2,1)}) custom-call(bf16[1,64,64,384]{3,2,1,0:T(8,128)(2,1)} %before_ref.1, bf16[1,64,64,384]{3,2,1,0:T(8,128)(2,1)} %before_ref.1, s32[64,64]{1,0:T(8,128)} %land_ref.1, f32[4,384]{1,0:T(4,128)} %gain_ref.3, ...), custom_call_target="tpu_custom_call" | custom-call | tf_op jit(solution)/shard_map/first_layer/pallas_call | solution.py:389
  36.4 2.2 %collective-permute-start = (bf16[64,4,512]{2,1,0:T(4,128)(2,1)}, bf16[64,4,512]{2,1,0:T(4,128)(2,1)S(1)}, u32[]{:S(2)}, u32[]{:S(2)}) collective-permute-start(bf16[64,4,512]{2,1,0:T(4,128)(2,1)} %get-tuple-element.9), channel_id=1, source_target_pairs={{1,0},{2,1},{3,2},{4,3},{5,4},{6,5},{7,6},{0,7},{9,8},{10,9},{11,1... | collective-permute-start | bytes 786440 | tf_op jit(solution)/shard_map/ppermute | solution.py:449
  38.6 0.0 collective-permute-start.1
  38.6 1.1 %fusion = (bf16[4,64,512]{2,1,0:T(8,128)(2,1)S(1)}, bf16[4,64,512]{2,1,0:T(8,128)(2,1)S(1)}) fusion(bf16[64,64,512]{2,1,0:T(8,128)(2,1)} %get-tuple-element.8.low_ref.high_ref.own_ref), kind=kLoop, calls=%fused_computation.2 | loop fusion | bytes 1048576 | tf_op jit(solution)/shard_map/slice | solution.py:452
  39.6 3.1 %collective-permute-done.low_right_ref.high_right_ref = bf16[64,4,512]{2,1,0:T(4,128)(2,1)S(1)} collective-permute-done((bf16[64,4,512]{2,1,0:T(4,128)(2,1)}, bf16[64,4,512]{2,1,0:T(4,128)(2,1)S(1)}, u32[]{:S(2)}, u32[]{:S(2)}) %collective-permute-start) | collective-permute-done | bytes 262176 | tf_op jit(solution)/shard_map/ppermute | solution.py:449
  42.8 0.0 copy-start
  42.8 3.0 %collective-permute-done.1.low_left_ref.high_left_ref = bf16[64,4,512]{2,1,0:T(4,128)(2,1)S(1)} collective-permute-done((bf16[64,4,512]{2,1,0:T(4,128)(2,1)}, bf16[64,4,512]{2,1,0:T(4,128)(2,1)S(1)}, u32[]{:S(2)}, u32[]{:S(2)}) %collective-permute-start.1) | collective-permute-done | bytes 262176 | tf_op jit(solution)/shard_map/ppermute | solution.py:448
  45.8 0.0 copy-start.1
  45.9 2.1 %collective-permute-start.2 = (bf16[4,72,512]{2,1,0:T(8,128)(2,1)S(1)}, bf16[4,72,512]{2,1,0:T(8,128)(2,1)S(1)}, u32[]{:S(2)}, u32[]{:S(2)}) collective-permute-start(bf16[4,72,512]{2,1,0:T(8,128)(2,1)S(1)} %pad_maximum_fusion), channel_id=1, source_target_pairs={{0,8},{8,16},{16,24},{24,32},{32,40},{40,48},{48,56},{56,64},{64,7... | collective-permute-start | bytes 884744 | tf_op jit(solution)/shard_map/ppermute | solution.py:451
  48.0 3.9 %collective-permute-start.3 = (bf16[4,72,512]{2,1,0:T(8,128)(2,1)S(1)}, bf16[4,72,512]{2,1,0:T(8,128)(2,1)S(1)}, u32[]{:S(2)}, u32[]{:S(2)}) collective-permute-start(bf16[4,72,512]{2,1,0:T(8,128)(2,1)S(1)} %pad_maximum_fusion.1), channel_id=1, source_target_pairs={{8,0},{16,8},{24,16},{32,24},{40,32},{48,40},{56,48},{64,56},{72,6... | collective-permute-start | bytes 884744 | tf_op jit(solution)/shard_map/ppermute | solution.py:452
  51.9 2.5 %collective-permute-done.2.above_ref = bf16[4,72,512]{2,1,0:T(8,128)(2,1)S(1)} collective-permute-done((bf16[4,72,512]{2,1,0:T(8,128)(2,1)S(1)}, bf16[4,72,512]{2,1,0:T(8,128)(2,1)S(1)}, u32[]{:S(2)}, u32[]{:S(2)}) %collective-permute-start.2) | collective-permute-done | bytes 294944 | tf_op jit(solution)/shard_map/ppermute | solution.py:451
  54.5 0.0 copy-start.2
  54.5 4.3 %collective-permute-done.3.below_ref = bf16[4,72,512]{2,1,0:T(8,128)(2,1)S(1)} collective-permute-done((bf16[4,72,512]{2,1,0:T(8,128)(2,1)S(1)}, bf16[4,72,512]{2,1,0:T(8,128)(2,1)S(1)}, u32[]{:S(2)}, u32[]{:S(2)}) %collective-permute-start.3) | collective-permute-done | bytes 294944 | tf_op jit(solution)/shard_map/ppermute | solution.py:452
  58.7 0.0 copy-done
  58.8 0.0 copy-done.1
  58.8 0.0 copy-done.2
  58.8 0.0 copy-start.3
  58.8 0.7 copy-done.3
  59.5 45.2 %second_layer.1 = bf16[1,64,64,384]{3,2,1,0:T(8,128)(2,1)} custom-call(bf16[64,64,512]{2,1,0:T(8,128)(2,1)} %get-tuple-element.8.low_ref.high_ref.own_ref, bf16[64,64,512]{2,1,0:T(8,128)(2,1)} %get-tuple-element.8.low_ref.high_ref.own_ref, bf16[64,4,512]{2,1,0:T(4,128)(2,1)} %copy-done, bf16[64,4,512]{2,1,0:T(4,128)(2,1)} %copy-done, ...), custom_call_target="tpu_custom_call" | custom-call | tf_op jit(solution)/shard_map/second_layer/pallas_call | solution.py:415
  (4 shorter events, 0.1 us)
Async XLA Ops:
  36.4 6.4 %collective-permute-start = (bf16[64,4,512]{2,1,0:T(4,128)(2,1)}, bf16[64,4,512]{2,1,0:T(4,128)(2,1)S(1)}, u32[]{:S(2)}, u32[]{:S(2)}) collective-permute-start(bf16[64,4,512]{2,1,0:T(4,128)(2,1)} %get-tuple-element.9), channel_id=1, source_target_pairs={{1,0},{2,1},{3,2},{4,3},{5,4},{6,5},{7,6},{0,7},{9,8},{10,9},{11,1... | collective-permute-start | bytes 786440 | tf_op jit(solution)/shard_map/ppermute | solution.py:449
  38.6 7.2 %collective-permute-start.1 = (bf16[64,4,512]{2,1,0:T(4,128)(2,1)}, bf16[64,4,512]{2,1,0:T(4,128)(2,1)S(1)}, u32[]{:S(2)}, u32[]{:S(2)}) collective-permute-start(bf16[64,4,512]{2,1,0:T(4,128)(2,1)} %get-tuple-element.10), channel_id=1, source_target_pairs={{0,1},{1,2},{2,3},{3,4},{4,5},{5,6},{6,7},{7,0},{8,9},{9,10},{10,1... | collective-permute-start | bytes 786440 | tf_op jit(solution)/shard_map/ppermute | solution.py:448
  42.8 16.0 %copy-start = (bf16[64,4,512]{2,1,0:T(4,128)(2,1)}, bf16[64,4,512]{2,1,0:T(4,128)(2,1)S(1)}, u32[]{:S(2)}) copy-start(bf16[64,4,512]{2,1,0:T(4,128)(2,1)S(1)} %collective-permute-done.low_right_ref.high_right_ref) | copy-start | bytes 786436
  45.8 13.0 %copy-start.1 = (bf16[64,4,512]{2,1,0:T(4,128)(2,1)}, bf16[64,4,512]{2,1,0:T(4,128)(2,1)S(1)}, u32[]{:S(2)}) copy-start(bf16[64,4,512]{2,1,0:T(4,128)(2,1)S(1)} %collective-permute-done.1.low_left_ref.high_left_ref) | copy-start | bytes 786436
  45.9 8.6 %collective-permute-start.2 = (bf16[4,72,512]{2,1,0:T(8,128)(2,1)S(1)}, bf16[4,72,512]{2,1,0:T(8,128)(2,1)S(1)}, u32[]{:S(2)}, u32[]{:S(2)}) collective-permute-start(bf16[4,72,512]{2,1,0:T(8,128)(2,1)S(1)} %pad_maximum_fusion), channel_id=1, source_target_pairs={{0,8},{8,16},{16,24},{24,32},{32,40},{40,48},{48,56},{56,64},{64,7... | collective-permute-start | bytes 884744 | tf_op jit(solution)/shard_map/ppermute | solution.py:451
  48.0 10.7 %collective-permute-start.3 = (bf16[4,72,512]{2,1,0:T(8,128)(2,1)S(1)}, bf16[4,72,512]{2,1,0:T(8,128)(2,1)S(1)}, u32[]{:S(2)}, u32[]{:S(2)}) collective-permute-start(bf16[4,72,512]{2,1,0:T(8,128)(2,1)S(1)} %pad_maximum_fusion.1), channel_id=1, source_target_pairs={{8,0},{16,8},{24,16},{32,24},{40,32},{48,40},{56,48},{64,56},{72,6... | collective-permute-start | bytes 884744 | tf_op jit(solution)/shard_map/ppermute | solution.py:452
  54.5 4.3 %copy-start.2 = (bf16[4,72,512]{2,1,0:T(8,128)(2,1)}, bf16[4,72,512]{2,1,0:T(8,128)(2,1)S(1)}, u32[]{:S(2)}) copy-start(bf16[4,72,512]{2,1,0:T(8,128)(2,1)S(1)} %collective-permute-done.2.above_ref) | copy-start | bytes 884740
  58.8 0.7 copy-start.3

commit v4 on v3

--- a/solution.py
+++ b/solution.py
@@ -19,6 +19,7 @@
 LOG2E = 1.4426950408889634
 QSCALE = LOG2E / (C // HEADS) ** 0.5
 BF = jnp.bfloat16
+GELU_SCALE = (2.0 / np.pi) ** 0.5
 UP_CHUNK = 256
 FINE = True
 LAG = 2
@@ -26,6 +27,7 @@
 AHEAD = 0.0
 COSTS = (22, 22, 18)
 F32 = jnp.float32
+GELU = BF
 
 
 WIDE = C + 128
@@ -56,6 +58,12 @@
     moved = values - center
     spread = jnp.mean(moved * moved, axis=-1, keepdims=True)
     return (moved * lax.rsqrt(spread + EPS) * gain).astype(BF)
+
+
+def gelu(x):
+    x = x.astype(GELU)
+    inner = x * (x * x * GELU(0.044715 * GELU_SCALE) + GELU(GELU_SCALE))
+    return (x * GELU(0.5) * (jnp.tanh(inner) + GELU(1.0))).astype(BF)
 
 
 def dot_nt(a, b):
@@ -149,7 +157,7 @@
 
     def up(at):
         lanes = pl.ds(at, UP_CHUNK)
-        hid_ref[:, lanes] = jax.nn.gelu(dot_nn(n_ref[...], up_ref[:, lanes]), approximate=True).astype(BF)
+        hid_ref[:, lanes] = gelu(dot_nn(n_ref[...], up_ref[:, lanes]))
 
     def down(part):
         rows = 8 * TOK // DOWN_PARTS

time: 105 us -> 101 us (0.962)
  Pallas kernels: 81.5 us -> 78.1 us
    pallas_call x1, Pallas kernels: 45.2 us -> 43.2 us  [second_layer(): pl.pallas_call(second_kernel, grid=(bands + 2,), in_specs=[pl.BlockSpec((...]
    pallas_call x1, Pallas kernels: 36.4 us -> 34.9 us  [first_layer(): pl.pallas_call(first_kernel, grid=(bands + 1,), in_specs=[pl.BlockSpec((1...]
where the time goes in v4:
time: 101 us
  Pallas kernels  78.1 us (77%)
  waiting for transfers between devices  12.9 us (13%)
  starting transfers between devices  8.24 us (8%)
  local copies, waits for them, and re-layouts  1.81 us (2%)
    pallas_call x1, Pallas kernels, second_layer(): pl.pallas_call(second_kernel, grid=(bands + 2,), in_specs=[pl.BlockSpec((...  43.2 us
    pallas_call x1, Pallas kernels, first_layer(): pl.pallas_call(first_kernel, grid=(bands + 1,), in_specs=[pl.BlockSpec((1...  34.9 us
    ppermute x1, waiting for transfers between devices, borders(): lax.ppermute(jnp.concatenate([part[:SHIFT] for part in (block, right, lef...  4.28 us
    ppermute x1, starting transfers between devices, borders(): lax.ppermute(jnp.concatenate([part[:SHIFT] for part in (block, right, lef...  3.9 us
    ppermute x1, waiting for transfers between devices, borders(): right = lax.ppermute(begin, 'lon', backward)  3.14 us
    ppermute x1, waiting for transfers between devices, borders(): left = lax.ppermute(end, 'lon', forward)  2.99 us
    ppermute x1, waiting for transfers between devices, borders(): lax.ppermute(jnp.concatenate([part[-SHIFT:] for part in (block, right, le...  2.54 us
    ppermute x1, starting transfers between devices, borders(): right = lax.ppermute(begin, 'lon', backward)  2.21 us
  transfers between devices with their start and end apart: 4, of which 4 were waited for; matrix products, arithmetic and copies ran while one was open for 1% of the time, Pallas kernels for 0%

profile of v4, /device:TPU:104, one launch (start us, length us, event | category | flops | bytes accessed | tf_op | source)
XLA Modules:
  0.0 101.2 jit_solution(3556468697999756809)
XLA Ops:
  0.0 34.9 %first_layer.1 = (bf16[64,64,512]{2,1,0:T(8,128)(2,1)}, bf16[64,4,512]{2,1,0:T(4,128)(2,1)}, bf16[64,4,512]{2,1,0:T(4,128)(2,1)}) custom-call(bf16[1,64,64,384]{3,2,1,0:T(8,128)(2,1)} %before_ref.1, bf16[1,64,64,384]{3,2,1,0:T(8,128)(2,1)} %before_ref.1, s32[64,64]{1,0:T(8,128)} %land_ref.1, f32[4,384]{1,0:T(4,128)} %gain_ref.3, ...), custom_call_target="tpu_custom_call" | custom-call | tf_op jit(solution)/shard_map/first_layer/pallas_call | solution.py:397
  34.9 2.2 %collective-permute-start = (bf16[64,4,512]{2,1,0:T(4,128)(2,1)}, bf16[64,4,512]{2,1,0:T(4,128)(2,1)S(1)}, u32[]{:S(2)}, u32[]{:S(2)}) collective-permute-start(bf16[64,4,512]{2,1,0:T(4,128)(2,1)} %get-tuple-element.9), channel_id=1, source_target_pairs={{1,0},{2,1},{3,2},{4,3},{5,4},{6,5},{7,6},{0,7},{9,8},{10,9},{11,1... | collective-permute-start | bytes 786440 | tf_op jit(solution)/shard_map/ppermute | solution.py:457
  37.1 0.0 collective-permute-start.1
  37.1 1.1 %fusion = (bf16[4,64,512]{2,1,0:T(8,128)(2,1)S(1)}, bf16[4,64,512]{2,1,0:T(8,128)(2,1)S(1)}) fusion(bf16[64,64,512]{2,1,0:T(8,128)(2,1)} %get-tuple-element.8.low_ref.high_ref.own_ref), kind=kLoop, calls=%fused_computation.2 | loop fusion | bytes 1048576 | tf_op jit(solution)/shard_map/slice | solution.py:460
  38.2 3.1 %collective-permute-done.low_right_ref.high_right_ref = bf16[64,4,512]{2,1,0:T(4,128)(2,1)S(1)} collective-permute-done((bf16[64,4,512]{2,1,0:T(4,128)(2,1)}, bf16[64,4,512]{2,1,0:T(4,128)(2,1)S(1)}, u32[]{:S(2)}, u32[]{:S(2)}) %collective-permute-start) | collective-permute-done | bytes 262176 | tf_op jit(solution)/shard_map/ppermute | solution.py:457
  41.3 0.0 copy-start
  41.3 3.0 %collective-permute-done.1.low_left_ref.high_left_ref = bf16[64,4,512]{2,1,0:T(4,128)(2,1)S(1)} collective-permute-done((bf16[64,4,512]{2,1,0:T(4,128)(2,1)}, bf16[64,4,512]{2,1,0:T(4,128)(2,1)S(1)}, u32[]{:S(2)}, u32[]{:S(2)}) %collective-permute-start.1) | collective-permute-done | bytes 262176 | tf_op jit(solution)/shard_map/ppermute | solution.py:456
  44.3 0.0 copy-start.1
  44.4 2.1 %collective-permute-start.2 = (bf16[4,72,512]{2,1,0:T(8,128)(2,1)S(1)}, bf16[4,72,512]{2,1,0:T(8,128)(2,1)S(1)}, u32[]{:S(2)}, u32[]{:S(2)}) collective-permute-start(bf16[4,72,512]{2,1,0:T(8,128)(2,1)S(1)} %pad_maximum_fusion), channel_id=1, source_target_pairs={{0,8},{8,16},{16,24},{24,32},{32,40},{40,48},{48,56},{56,64},{64,7... | collective-permute-start | bytes 884744 | tf_op jit(solution)/shard_map/ppermute | solution.py:459
  46.5 3.9 %collective-permute-start.3 = (bf16[4,72,512]{2,1,0:T(8,128)(2,1)S(1)}, bf16[4,72,512]{2,1,0:T(8,128)(2,1)S(1)}, u32[]{:S(2)}, u32[]{:S(2)}) collective-permute-start(bf16[4,72,512]{2,1,0:T(8,128)(2,1)S(1)} %pad_maximum_fusion.1), channel_id=1, source_target_pairs={{8,0},{16,8},{24,16},{32,24},{40,32},{48,40},{56,48},{64,56},{72,6... | collective-permute-start | bytes 884744 | tf_op jit(solution)/shard_map/ppermute | solution.py:460
  50.5 2.5 %collective-permute-done.2.above_ref = bf16[4,72,512]{2,1,0:T(8,128)(2,1)S(1)} collective-permute-done((bf16[4,72,512]{2,1,0:T(8,128)(2,1)S(1)}, bf16[4,72,512]{2,1,0:T(8,128)(2,1)S(1)}, u32[]{:S(2)}, u32[]{:S(2)}) %collective-permute-start.2) | collective-permute-done | bytes 294944 | tf_op jit(solution)/shard_map/ppermute | solution.py:459
  53.0 0.0 copy-start.2
  53.0 4.3 %collective-permute-done.3.below_ref = bf16[4,72,512]{2,1,0:T(8,128)(2,1)S(1)} collective-permute-done((bf16[4,72,512]{2,1,0:T(8,128)(2,1)S(1)}, bf16[4,72,512]{2,1,0:T(8,128)(2,1)S(1)}, u32[]{:S(2)}, u32[]{:S(2)}) %collective-permute-start.3) | collective-permute-done | bytes 294944 | tf_op jit(solution)/shard_map/ppermute | solution.py:460
  57.3 0.0 copy-done
  57.3 0.0 copy-done.1
  57.3 0.0 copy-done.2
  57.3 0.0 copy-start.3
  57.3 0.7 copy-done.3
  58.0 43.2 %second_layer.1 = bf16[1,64,64,384]{3,2,1,0:T(8,128)(2,1)} custom-call(bf16[64,64,512]{2,1,0:T(8,128)(2,1)} %get-tuple-element.8.low_ref.high_ref.own_ref, bf16[64,64,512]{2,1,0:T(8,128)(2,1)} %get-tuple-element.8.low_ref.high_ref.own_ref, bf16[64,4,512]{2,1,0:T(4,128)(2,1)} %copy-done, bf16[64,4,512]{2,1,0:T(4,128)(2,1)} %copy-done, ...), custom_call_target="tpu_custom_call" | custom-call | tf_op jit(solution)/shard_map/second_layer/pallas_call | solution.py:423
  (4 shorter events, 0.1 us)
Async XLA Ops:
  34.9 6.4 %collective-permute-start = (bf16[64,4,512]{2,1,0:T(4,128)(2,1)}, bf16[64,4,512]{2,1,0:T(4,128)(2,1)S(1)}, u32[]{:S(2)}, u32[]{:S(2)}) collective-permute-start(bf16[64,4,512]{2,1,0:T(4,128)(2,1)} %get-tuple-element.9), channel_id=1, source_target_pairs={{1,0},{2,1},{3,2},{4,3},{5,4},{6,5},{7,6},{0,7},{9,8},{10,9},{11,1... | collective-permute-start | bytes 786440 | tf_op jit(solution)/shard_map/ppermute | solution.py:457
  37.1 7.2 %collective-permute-start.1 = (bf16[64,4,512]{2,1,0:T(4,128)(2,1)}, bf16[64,4,512]{2,1,0:T(4,128)(2,1)S(1)}, u32[]{:S(2)}, u32[]{:S(2)}) collective-permute-start(bf16[64,4,512]{2,1,0:T(4,128)(2,1)} %get-tuple-element.10), channel_id=1, source_target_pairs={{0,1},{1,2},{2,3},{3,4},{4,5},{5,6},{6,7},{7,0},{8,9},{9,10},{10,1... | collective-permute-start | bytes 786440 | tf_op jit(solution)/shard_map/ppermute | solution.py:456
  41.3 16.0 %copy-start = (bf16[64,4,512]{2,1,0:T(4,128)(2,1)}, bf16[64,4,512]{2,1,0:T(4,128)(2,1)S(1)}, u32[]{:S(2)}) copy-start(bf16[64,4,512]{2,1,0:T(4,128)(2,1)S(1)} %collective-permute-done.low_right_ref.high_right_ref) | copy-start | bytes 786436
  44.3 13.0 %copy-start.1 = (bf16[64,4,512]{2,1,0:T(4,128)(2,1)}, bf16[64,4,512]{2,1,0:T(4,128)(2,1)S(1)}, u32[]{:S(2)}) copy-start(bf16[64,4,512]{2,1,0:T(4,128)(2,1)S(1)} %collective-permute-done.1.low_left_ref.high_left_ref) | copy-start | bytes 786436
  44.4 8.6 %collective-permute-start.2 = (bf16[4,72,512]{2,1,0:T(8,128)(2,1)S(1)}, bf16[4,72,512]{2,1,0:T(8,128)(2,1)S(1)}, u32[]{:S(2)}, u32[]{:S(2)}) collective-permute-start(bf16[4,72,512]{2,1,0:T(8,128)(2,1)S(1)} %pad_maximum_fusion), channel_id=1, source_target_pairs={{0,8},{8,16},{16,24},{24,32},{32,40},{40,48},{48,56},{56,64},{64,7... | collective-permute-start | bytes 884744 | tf_op jit(solution)/shard_map/ppermute | solution.py:459
  46.5 10.7 %collective-permute-start.3 = (bf16[4,72,512]{2,1,0:T(8,128)(2,1)S(1)}, bf16[4,72,512]{2,1,0:T(8,128)(2,1)S(1)}, u32[]{:S(2)}, u32[]{:S(2)}) collective-permute-start(bf16[4,72,512]{2,1,0:T(8,128)(2,1)S(1)} %pad_maximum_fusion.1), channel_id=1, source_target_pairs={{8,0},{16,8},{24,16},{32,24},{40,32},{48,40},{56,48},{64,56},{72,6... | collective-permute-start | bytes 884744 | tf_op jit(solution)/shard_map/ppermute | solution.py:460
  53.0 4.3 %copy-start.2 = (bf16[4,72,512]{2,1,0:T(8,128)(2,1)}, bf16[4,72,512]{2,1,0:T(8,128)(2,1)S(1)}, u32[]{:S(2)}) copy-start(bf16[4,72,512]{2,1,0:T(8,128)(2,1)S(1)} %collective-permute-done.2.above_ref) | copy-start | bytes 884740
  57.3 0.7 copy-start.3

commit v5 on v4

--- a/solution.py
+++ b/solution.py
@@ -91,20 +91,22 @@
 
 
 def weigh_head(s_ref, p_ref, pair, head):
-    side = lax.broadcasted_iota(jnp.int32, (1, 128), 1) < TOK
+    side = (lax.broadcasted_iota(jnp.int32, (TOK, 128), 1) < TOK).astype(F32)
     s = s_ref[pair % 2, head]
-    e = jnp.exp2(s - jnp.max(s, axis=0, keepdims=True))
-    inv = 1.0 / jnp.sum(e, axis=0, keepdims=True)
+    e = jnp.exp2(s - jnp.max(s, axis=0, keepdims=True)).astype(BF)
     lanes = pl.ds(head % 2 * 128, 128)
-    p_ref[pair % 2, head // 2, :TOK, lanes] = (e * jnp.where(side, inv, 0.0)).astype(BF)
-    p_ref[pair % 2, head // 2, TOK:, lanes] = (e * jnp.where(side, 0.0, inv)).astype(BF)
+    p_ref[pair % 2, head // 2, :TOK, lanes] = e * side.astype(BF)
+    p_ref[pair % 2, head // 2, TOK:, lanes] = e * (1.0 - side).astype(BF)
 
 
 def mix_two(vt_ref, p_ref, ot_ref, pair, two):
     here = pl.ds(pair * 128, 128)
-    mixed = dot_nn(vt_ref[pl.ds(two * 64, 64), here], p_ref[pair % 2, two])
-    ot_ref[pl.ds(two * 64, 32), here] = mixed[:32, :128]
-    ot_ref[pl.ds(two * 64 + 32, 32), here] = mixed[32:, 128:]
+    rows = jnp.concatenate([vt_ref[pl.ds(two * 64, 64), here], jnp.ones((16, 128), BF)], axis=0)
+    mixed = dot_nn(rows, p_ref[pair % 2, two])
+    inv = 1.0 / mixed[64:72]
+    inv = jnp.concatenate([inv] * 4, axis=0)
+    ot_ref[pl.ds(two * 64, 32), here] = mixed[:32, :128] * inv[:, :128]
+    ot_ref[pl.ds(two * 64 + 32, 32), here] = mixed[32:64, 128:] * inv[:, 128:]
 
 
 def attend_stages(qt_ref, k_ref, vt_ref, bias_ref, s_ref, p_ref, ot_ref, mask_ref, ocean, pairs):

time: 101 us -> 101 us (level)
  no operation moved by 1% of the time
where the time goes in v5:
time: 101 us; the launch traced here: 100 us
  Pallas kernels  77.3 us (77%)
  waiting for transfers between devices  13 us (13%)
  starting transfers between devices  8.22 us (8%)
  local copies, waits for them, and re-layouts  1.81 us (2%)
    pallas_call x1, Pallas kernels, second_layer(): pl.pallas_call(second_kernel, grid=(bands + 2,), in_specs=[pl.BlockSpec((...  42.6 us
    pallas_call x1, Pallas kernels, first_layer(): pl.pallas_call(first_kernel, grid=(bands + 1,), in_specs=[pl.BlockSpec((1...  34.7 us
    ppermute x1, waiting for transfers between devices, borders(): lax.ppermute(jnp.concatenate([part[:SHIFT] for part in (block, right, lef...  4.28 us
    ppermute x1, starting transfers between devices, borders(): lax.ppermute(jnp.concatenate([part[:SHIFT] for part in (block, right, lef...  3.89 us
    ppermute x1, waiting for transfers between devices, borders(): right = lax.ppermute(begin, 'lon', backward)  3.14 us
    ppermute x1, waiting for transfers between devices, borders(): left = lax.ppermute(end, 'lon', forward)  2.99 us
    ppermute x1, waiting for transfers between devices, borders(): lax.ppermute(jnp.concatenate([part[-SHIFT:] for part in (block, right, le...  2.54 us
    ppermute x1, starting transfers between devices, borders(): right = lax.ppermute(begin, 'lon', backward)  2.2 us
  transfers between devices with their start and end apart: 4, of which 4 were waited for; matrix products, arithmetic and copies ran while one was open for 1% of the time, Pallas kernels for 0%

profile of v5, /device:TPU:104, one launch (start us, length us, event | category | flops | bytes accessed | tf_op | source)
XLA Modules:
  0.0 100.4 jit_solution(4020651602503035159)
XLA Ops:
  0.0 34.7 %first_layer.1 = (bf16[64,64,512]{2,1,0:T(8,128)(2,1)}, bf16[64,4,512]{2,1,0:T(4,128)(2,1)}, bf16[64,4,512]{2,1,0:T(4,128)(2,1)}) custom-call(bf16[1,64,64,384]{3,2,1,0:T(8,128)(2,1)} %before_ref.1, bf16[1,64,64,384]{3,2,1,0:T(8,128)(2,1)} %before_ref.1, s32[64,64]{1,0:T(8,128)} %land_ref.1, f32[4,384]{1,0:T(4,128)} %gain_ref.3, ...), custom_call_target="tpu_custom_call" | custom-call | tf_op jit(solution)/shard_map/first_layer/pallas_call | solution.py:399
  34.7 2.2 %collective-permute-start = (bf16[64,4,512]{2,1,0:T(4,128)(2,1)}, bf16[64,4,512]{2,1,0:T(4,128)(2,1)S(1)}, u32[]{:S(2)}, u32[]{:S(2)}) collective-permute-start(bf16[64,4,512]{2,1,0:T(4,128)(2,1)} %get-tuple-element.9), channel_id=1, source_target_pairs={{1,0},{2,1},{3,2},{4,3},{5,4},{6,5},{7,6},{0,7},{9,8},{10,9},{11,1... | collective-permute-start | bytes 786440 | tf_op jit(solution)/shard_map/ppermute | solution.py:459
  36.9 0.0 collective-permute-start.1
  36.9 1.1 %fusion = (bf16[4,64,512]{2,1,0:T(8,128)(2,1)S(1)}, bf16[4,64,512]{2,1,0:T(8,128)(2,1)S(1)}) fusion(bf16[64,64,512]{2,1,0:T(8,128)(2,1)} %get-tuple-element.8.low_ref.high_ref.own_ref), kind=kLoop, calls=%fused_computation.2 | loop fusion | bytes 1048576 | tf_op jit(solution)/shard_map/slice | solution.py:462
  38.0 3.1 %collective-permute-done.low_right_ref.high_right_ref = bf16[64,4,512]{2,1,0:T(4,128)(2,1)S(1)} collective-permute-done((bf16[64,4,512]{2,1,0:T(4,128)(2,1)}, bf16[64,4,512]{2,1,0:T(4,128)(2,1)S(1)}, u32[]{:S(2)}, u32[]{:S(2)}) %collective-permute-start) | collective-permute-done | bytes 262176 | tf_op jit(solution)/shard_map/ppermute | solution.py:459
  41.1 0.0 copy-start
  41.1 3.0 %collective-permute-done.1.low_left_ref.high_left_ref = bf16[64,4,512]{2,1,0:T(4,128)(2,1)S(1)} collective-permute-done((bf16[64,4,512]{2,1,0:T(4,128)(2,1)}, bf16[64,4,512]{2,1,0:T(4,128)(2,1)S(1)}, u32[]{:S(2)}, u32[]{:S(2)}) %collective-permute-start.1) | collective-permute-done | bytes 262176 | tf_op jit(solution)/shard_map/ppermute | solution.py:458
  44.1 0.0 copy-start.1
  44.2 2.1 %collective-permute-start.2 = (bf16[4,72,512]{2,1,0:T(8,128)(2,1)S(1)}, bf16[4,72,512]{2,1,0:T(8,128)(2,1)S(1)}, u32[]{:S(2)}, u32[]{:S(2)}) collective-permute-start(bf16[4,72,512]{2,1,0:T(8,128)(2,1)S(1)} %pad_maximum_fusion), channel_id=1, source_target_pairs={{0,8},{8,16},{16,24},{24,32},{32,40},{40,48},{48,56},{56,64},{64,7... | collective-permute-start | bytes 884744 | tf_op jit(solution)/shard_map/ppermute | solution.py:461
  46.4 3.9 %collective-permute-start.3 = (bf16[4,72,512]{2,1,0:T(8,128)(2,1)S(1)}, bf16[4,72,512]{2,1,0:T(8,128)(2,1)S(1)}, u32[]{:S(2)}, u32[]{:S(2)}) collective-permute-start(bf16[4,72,512]{2,1,0:T(8,128)(2,1)S(1)} %pad_maximum_fusion.1), channel_id=1, source_target_pairs={{8,0},{16,8},{24,16},{32,24},{40,32},{48,40},{56,48},{64,56},{72,6... | collective-permute-start | bytes 884744 | tf_op jit(solution)/shard_map/ppermute | solution.py:462
  50.3 2.5 %collective-permute-done.2.above_ref = bf16[4,72,512]{2,1,0:T(8,128)(2,1)S(1)} collective-permute-done((bf16[4,72,512]{2,1,0:T(8,128)(2,1)S(1)}, bf16[4,72,512]{2,1,0:T(8,128)(2,1)S(1)}, u32[]{:S(2)}, u32[]{:S(2)}) %collective-permute-start.2) | collective-permute-done | bytes 294944 | tf_op jit(solution)/shard_map/ppermute | solution.py:461
  52.8 0.0 copy-start.2
  52.8 4.3 %collective-permute-done.3.below_ref = bf16[4,72,512]{2,1,0:T(8,128)(2,1)S(1)} collective-permute-done((bf16[4,72,512]{2,1,0:T(8,128)(2,1)S(1)}, bf16[4,72,512]{2,1,0:T(8,128)(2,1)S(1)}, u32[]{:S(2)}, u32[]{:S(2)}) %collective-permute-start.3) | collective-permute-done | bytes 294944 | tf_op jit(solution)/shard_map/ppermute | solution.py:462
  57.1 0.0 copy-done
  57.1 0.0 copy-done.1
  57.1 0.0 copy-done.2
  57.1 0.0 copy-start.3
  57.1 0.7 copy-done.3
  57.8 42.6 %second_layer.1 = bf16[1,64,64,384]{3,2,1,0:T(8,128)(2,1)} custom-call(bf16[64,64,512]{2,1,0:T(8,128)(2,1)} %get-tuple-element.8.low_ref.high_ref.own_ref, bf16[64,64,512]{2,1,0:T(8,128)(2,1)} %get-tuple-element.8.low_ref.high_ref.own_ref, bf16[64,4,512]{2,1,0:T(4,128)(2,1)} %copy-done, bf16[64,4,512]{2,1,0:T(4,128)(2,1)} %copy-done, ...), custom_call_target="tpu_custom_call" | custom-call | tf_op jit(solution)/shard_map/second_layer/pallas_call | solution.py:425
  (4 shorter events, 0.1 us)
Async XLA Ops:
  34.7 6.4 %collective-permute-start = (bf16[64,4,512]{2,1,0:T(4,128)(2,1)}, bf16[64,4,512]{2,1,0:T(4,128)(2,1)S(1)}, u32[]{:S(2)}, u32[]{:S(2)}) collective-permute-start(bf16[64,4,512]{2,1,0:T(4,128)(2,1)} %get-tuple-element.9), channel_id=1, source_target_pairs={{1,0},{2,1},{3,2},{4,3},{5,4},{6,5},{7,6},{0,7},{9,8},{10,9},{11,1... | collective-permute-start | bytes 786440 | tf_op jit(solution)/shard_map/ppermute | solution.py:459
  36.9 7.2 %collective-permute-start.1 = (bf16[64,4,512]{2,1,0:T(4,128)(2,1)}, bf16[64,4,512]{2,1,0:T(4,128)(2,1)S(1)}, u32[]{:S(2)}, u32[]{:S(2)}) collective-permute-start(bf16[64,4,512]{2,1,0:T(4,128)(2,1)} %get-tuple-element.10), channel_id=1, source_target_pairs={{0,1},{1,2},{2,3},{3,4},{4,5},{5,6},{6,7},{7,0},{8,9},{9,10},{10,1... | collective-permute-start | bytes 786440 | tf_op jit(solution)/shard_map/ppermute | solution.py:458
  41.1 16.0 %copy-start = (bf16[64,4,512]{2,1,0:T(4,128)(2,1)}, bf16[64,4,512]{2,1,0:T(4,128)(2,1)S(1)}, u32[]{:S(2)}) copy-start(bf16[64,4,512]{2,1,0:T(4,128)(2,1)S(1)} %collective-permute-done.low_right_ref.high_right_ref) | copy-start | bytes 786436
  44.1 13.0 %copy-start.1 = (bf16[64,4,512]{2,1,0:T(4,128)(2,1)}, bf16[64,4,512]{2,1,0:T(4,128)(2,1)S(1)}, u32[]{:S(2)}) copy-start(bf16[64,4,512]{2,1,0:T(4,128)(2,1)S(1)} %collective-permute-done.1.low_left_ref.high_left_ref) | copy-start | bytes 786436
  44.2 8.6 %collective-permute-start.2 = (bf16[4,72,512]{2,1,0:T(8,128)(2,1)S(1)}, bf16[4,72,512]{2,1,0:T(8,128)(2,1)S(1)}, u32[]{:S(2)}, u32[]{:S(2)}) collective-permute-start(bf16[4,72,512]{2,1,0:T(8,128)(2,1)S(1)} %pad_maximum_fusion), channel_id=1, source_target_pairs={{0,8},{8,16},{16,24},{24,32},{32,40},{40,48},{48,56},{56,64},{64,7... | collective-permute-start | bytes 884744 | tf_op jit(solution)/shard_map/ppermute | solution.py:461
  46.4 10.7 %collective-permute-start.3 = (bf16[4,72,512]{2,1,0:T(8,128)(2,1)S(1)}, bf16[4,72,512]{2,1,0:T(8,128)(2,1)S(1)}, u32[]{:S(2)}, u32[]{:S(2)}) collective-permute-start(bf16[4,72,512]{2,1,0:T(8,128)(2,1)S(1)} %pad_maximum_fusion.1), channel_id=1, source_target_pairs={{8,0},{16,8},{24,16},{32,24},{40,32},{48,40},{56,48},{64,56},{72,6... | collective-permute-start | bytes 884744 | tf_op jit(solution)/shard_map/ppermute | solution.py:462
  52.8 4.3 %copy-start.2 = (bf16[4,72,512]{2,1,0:T(8,128)(2,1)}, bf16[4,72,512]{2,1,0:T(8,128)(2,1)S(1)}, u32[]{:S(2)}) copy-start(bf16[4,72,512]{2,1,0:T(8,128)(2,1)S(1)} %collective-permute-done.2.above_ref) | copy-start | bytes 884740
  57.1 0.7 copy-start.3
